TPU v7x, 512 devices: a whole 4x8x8 slice. The times are simulated.
512 devices in a mesh: snap: 32 (over z, x), vert: 16 (over y, core).
Axes of the slice: x: 4, y: 8, z: 8, core: 2. Of those that a mesh axis runs over, the one named last changes fastest.
Arguments:
- features: bfloat16 [32, 4096, 512], P('snap', 'vert'), may hold values from -6 to 6
- tile_values: bfloat16 [32, 32, 12, 128, 128], P('snap', 'vert'), may hold values from -0.21875 to 0.21875
- tile_column: int32 [32, 32, 12], P('snap', 'vert'), may hold values from 0 to 31
- tile_count: int32 [32, 32], P('snap', 'vert'), may hold values from 1 to 12, 192 in all within a row
- message_one: bfloat16 [512, 512], replicated, may hold values from -0.25 to 0.25
- root_one: bfloat16 [512, 512], replicated, may hold values from -0.25 to 0.25
- time_taps: float32 [16, 512], replicated, may hold values from -1.5 to 1.5
- message_two: bfloat16 [512, 512], replicated, may hold values from -0.25 to 0.25
- root_two: bfloat16 [512, 512], replicated, may hold values from -0.25 to 0.25
Outputs:
- embedding: bfloat16 [32, 4096, 512], P('snap', 'vert')
Inputs may be any that keep to these rules, and one draw needn't show every extreme that they name: `tile_count`: over one snapshot the counts sum to 192, and some row block has 12 live slots; slots at or past the count are ignored. `tile_column`: blocks may repeat within a row block's list.
All inputs are finite; a program needn't handle non-finite values.
Results may differ from a plain program's by a relative error of at most 0.0064.
Values may be sent and summed in bfloat16 or wider, within the bound.
No kernel may reach another device: no remote copies, remote signals or barrier semaphores. Data moves between devices by JAX's collectives and lax.ppermute only.
A program may use at most 64 MiB of HBM per device.

v0:
```python
import functools

import jax
import jax.numpy as jnp
from jax import lax
from jax.experimental import pallas as pl
from jax.experimental.pallas import tpu as pltpu
from jax.sharding import PartitionSpec as P

TILE = 128
TAPS = 16
RING = 8
SMEM = pl.BlockSpec(memory_space=pltpu.SMEM)
VMEM = pl.BlockSpec(memory_space=pltpu.VMEM)


def call(kernel, outs, operands, specs, flops, moved, aliases={}, scratch=()):
    return pl.pallas_call(
        kernel,
        out_shape=outs,
        in_specs=specs,
        out_specs=jax.tree.map(lambda _: VMEM, outs),
        scratch_shapes=scratch,
        input_output_aliases=aliases,
        cost_estimate=pl.CostEstimate(flops=flops, bytes_accessed=moved, transcendentals=0),
        compiler_params=pltpu.CompilerParams(vmem_limit_bytes=16 << 20),
    )(*operands)


def plan_kernel(slots, where, own, partner, plan):
    y, core = where[0] // 2, where[0] % 2
    lists = 2 * RING
    for i in range(lists):
        plan[i] = 0
    for side, table in enumerate((own, partner)):
        for r in range(2):

            @pl.loop(0, table[r * (slots + 1) + slots])
            def _(k):
                column = table[r * (slots + 1) + k]
                near = lax.rem(column // 4 - y + RING, RING) * 2 + side

                @pl.when(lax.rem(column // 2, 2) == core)
                def _():
                    filled = plan[near]
                    plan[lists + near * 2 * slots + filled] = (r * slots + k) * 2 + lax.rem(
                        column, 2
                    )
                    plan[near] = filled + 1


def add_tiles(plan, pieces, tiles, sums):
    for near, piece in pieces:
        for side in tiles:
            slots = tiles[side].shape[0] // 2
            index = near * 2 + side

            @pl.loop(0, plan[index])
            def _(i):
                entry = plan[2 * RING + index * 2 * slots + i]
                half, slot = lax.rem(entry, 2), entry // 2
                rows = pl.ds(pl.multiple_of(slot // slots * TILE, TILE), TILE)
                block = pl.ds(pl.multiple_of(half * TILE, TILE), TILE)
                sums[side][rows, :] += jnp.dot(
                    tiles[side][slot], piece[block, :], preferred_element_type=jnp.float32
                )


def early_kernel(plan, p0, p1, p2, p6, p7, own_tiles, other_tiles, w_root, mine, theirs, root):
    mine[...] = jnp.zeros_like(mine)
    theirs[...] = jnp.zeros_like(theirs)
    pieces = ((0, p0), (1, p1), (7, p7), (2, p2), (6, p6))
    add_tiles(plan, pieces, {0: own_tiles, 1: other_tiles}, {0: mine, 1: theirs})
    root[...] = jnp.dot(p0[...], w_root[...], preferred_element_type=jnp.float32)


def late_kernel(plan, p3, p4, p5, tiles, sums_in, sums, *, side):
    sums[...] = sums_in[...]
    add_tiles(plan, ((3, p3), (4, p4), (5, p5)), {side: tiles}, {side: sums})


def last_kernel(mine, received, root, w_message, out):
    total = (mine[...] + received[...]).astype(jnp.bfloat16)
    full = jnp.dot(total, w_message[...], preferred_element_type=jnp.float32) + root[...]
    out[...] = jnp.maximum(full, 0.0).astype(jnp.bfloat16)


def moves(up, down):
    return [(2 * y, (2 * y + 2 * up) % (2 * RING)) for y in range(RING)] + [
        (2 * y + 1, (2 * y + 2 * down) % (2 * RING) + 1) for y in range(RING)
    ]


def shift(x, distance):
    return lax.ppermute(x, "vert", moves(distance, distance))


def swap(x):
    return lax.ppermute(x, "vert", [(v, v ^ 1) for v in range(2 * RING)])


def ring_gather(own):
    first = lax.rem(lax.axis_index("vert"), 2) == 0
    up2, down2 = shift(own, 2), shift(own, -2)
    up1, down1 = shift(own, 1), shift(own, -1)
    up3, down3 = shift(up2, 1), shift(down2, -1)
    across = lax.ppermute(jnp.where(first, up2, down2), "vert", moves(2, -2))
    return (own, down1, down2, down3, across, up3, up2, up1)


def graph_layer(pieces, own_tiles, other_tiles, plan, w_message, w_root):
    own = pieces[0]
    rows, width = own.shape
    sums = jax.ShapeDtypeStruct((rows, width), jnp.float32)
    area = rows * width
    dense = 2 * area * width
    mine, theirs, root = call(
        early_kernel,
        (sums, sums, sums),
        (plan, own, pieces[1], pieces[2], pieces[6], pieces[7], own_tiles, other_tiles, w_root),
        [SMEM] + [VMEM] * 8,
        4 * dense,
        24 * area,
    )
    late = pieces[3:6]

    def finish(side, tiles, partial):
        return call(
            functools.partial(late_kernel, side=side),
            sums,
            (plan, *late, tiles, partial),
            [SMEM] + [VMEM] * 5,
            dense,
            8 * area,
            aliases={5: 0},
        )

    received = swap(finish(1, other_tiles, theirs))
    mine = finish(0, own_tiles, mine)
    return call(
        last_kernel,
        jax.ShapeDtypeStruct((rows, width), jnp.bfloat16),
        (mine, received, root, w_message),
        [VMEM] * 4,
        dense,
        14 * area,
    )


def filter_kernel(hidden, taps, out):
    steps = hidden.shape[0]
    for t in range(steps):
        acc = taps[0:1, :] * hidden[t].astype(jnp.float32)
        for j in range(1, min(TAPS - 1, t) + 1):
            acc = acc + taps[j : j + 1, :] * hidden[t - j].astype(jnp.float32)
        out[t] = acc.astype(jnp.bfloat16)


def temporal(hidden, taps):
    rows, width = hidden.shape
    steps = lax.axis_size("snap")
    split = hidden.reshape(steps, rows // steps, width)
    by_vertex = lax.all_to_all(split, "snap", split_axis=0, concat_axis=0)
    mixed = call(
        filter_kernel,
        jax.ShapeDtypeStruct(by_vertex.shape, jnp.bfloat16),
        (by_vertex, taps),
        [VMEM] * 2,
        32 * rows * width,
        4 * rows * width,
    )
    returned = lax.all_to_all(mixed, "snap", split_axis=0, concat_axis=0)
    return returned.reshape(rows, width)


def shards(
    features,
    tile_values,
    tile_column,
    tile_count,
    message_one,
    root_one,
    time_taps,
    message_two,
    root_two,
):
    slots = tile_column.shape[2]
    own_tiles = tile_values[0].reshape(2 * slots, TILE, TILE)
    table = jnp.concatenate([tile_column[0], tile_count[0][:, None]], 1).reshape(-1)
    pieces = ring_gather(features[0])
    other_tiles, other_table = swap(own_tiles), swap(table)
    plan = pl.pallas_call(
        functools.partial(plan_kernel, slots),
        out_shape=jax.ShapeDtypeStruct((2 * RING * (2 * slots + 1),), jnp.int32),
        in_specs=[SMEM] * 3,
        out_specs=SMEM,
        cost_estimate=pl.CostEstimate(flops=1000, bytes_accessed=4000, transcendentals=0),
        name="plan",
    )(lax.axis_index("vert").reshape(1), table, other_table)
    hidden = graph_layer(pieces, own_tiles, other_tiles, plan, message_one, root_one)
    mixed = temporal(hidden, time_taps)
    pieces = ring_gather(mixed)
    out = graph_layer(pieces, own_tiles, other_tiles, plan, message_two, root_two)
    return out[None]


def solution(mesh):
    return jax.shard_map(
        shards,
        mesh=mesh,
        in_specs=(
            P("snap", "vert", None),
            P("snap", "vert", None, None, None),
            P("snap", "vert", None),
            P("snap", "vert"),
            P(),
            P(),
            P(),
            P(),
            P(),
        ),
        out_specs=P("snap", "vert", None),
        check_vma=False,
    )
```

profile of v0, /device:TPU:1, one launch (start us, length us, event | category | flops | bytes accessed | tf_op | source)
XLA Modules:
  0.0 139.2 jit_solution(10940184195499078037)
XLA Ops:
  0.0 8.9 %collective-permute-start.8 = (bf16[24,128,128]{2,1,0:T(8,128)(2,1)}, bf16[24,128,128]{2,1,0:T(8,128)(2,1)S(1)}, u32[]{:S(2)}, u32[]{:S(2)}) collective-permute-start(bf16[24,128,128]{2,1,0:T(8,128)(2,1)} %bitcast.8), channel_id=1, source_target_pairs={{0,1},{1,0},{2,3},{3,2},{4,5},{5,4},{6,7},{7,6},{8,9},{9,8},{10,11... | collective-permute-start | bytes 2359304 | tf_op jit(solution)/shard_map/ppermute | solution.py:99
  8.9 1.9 %collective-permute-start.1 = (bf16[256,512]{1,0:T(8,128)(2,1)}, bf16[256,512]{1,0:T(8,128)(2,1)S(1)}, u32[]{:S(2)}, u32[]{:S(2)}) collective-permute-start(bf16[256,512]{1,0:T(8,128)(2,1)} %bitcast.19), channel_id=1, source_target_pairs={{0,12},{2,14},{4,0},{6,2},{8,4},{10,6},{12,8},{14,10},{1,13},{3,15... | collective-permute-start | bytes 786440 | tf_op jit(solution)/shard_map/ppermute | solution.py:95
  10.8 4.3 %collective-permute-start.3 = (bf16[256,512]{1,0:T(8,128)(2,1)}, bf16[256,512]{1,0:T(8,128)(2,1)S(1)}, u32[]{:S(2)}, u32[]{:S(2)}) collective-permute-start(bf16[256,512]{1,0:T(8,128)(2,1)} %bitcast.20), channel_id=1, source_target_pairs={{0,4},{2,6},{4,8},{6,10},{8,12},{10,14},{12,0},{14,2},{1,5},{3,7},... | collective-permute-start | bytes 786440 | tf_op jit(solution)/shard_map/ppermute | solution.py:95
  15.1 1.9 %collective-permute-start.6 = (bf16[256,512]{1,0:T(8,128)(2,1)}, bf16[256,512]{1,0:T(8,128)(2,1)S(1)}, u32[]{:S(2)}, u32[]{:S(2)}) collective-permute-start(bf16[256,512]{1,0:T(8,128)(2,1)} %bitcast.21), channel_id=1, source_target_pairs={{0,14},{2,0},{4,2},{6,4},{8,6},{10,8},{12,10},{14,12},{1,15},{3,1}... | collective-permute-start | bytes 786440 | tf_op jit(solution)/shard_map/ppermute | solution.py:95
  17.0 3.4 %collective-permute-start.7 = (bf16[256,512]{1,0:T(8,128)(2,1)}, bf16[256,512]{1,0:T(8,128)(2,1)S(1)}, u32[]{:S(2)}, u32[]{:S(2)}) collective-permute-start(bf16[256,512]{1,0:T(8,128)(2,1)} %bitcast.22), channel_id=1, source_target_pairs={{0,2},{2,4},{4,6},{6,8},{8,10},{10,12},{12,14},{14,0},{1,3},{3,5},... | collective-permute-start | bytes 786440 | tf_op jit(solution)/shard_map/ppermute | solution.py:95
  20.4 0.7 copy.14
  21.1 0.8 pad_add_fusion
  21.9 0.1 reshape.13.own
  22.0 0.5 collective-permute-done.1.p2
  22.5 0.0 copy-done.9
  22.5 3.0 %collective-permute-start = (s32[26]{0:T(128)S(1)}, s32[26]{0:T(128)S(1)}, u32[]{:S(2)}, u32[]{:S(2)}) collective-permute-start(s32[26]{0:T(128)S(1)} %reshape.13.own), channel_id=1, source_target_pairs={{0,1},{1,0},{2,3},{3,2},{4,5},{5,4},{6,7},{7,6},{8,9},{9,8},{10,11... | collective-permute-start | bytes 320 | tf_op jit(solution)/shard_map/ppermute | solution.py:99
  25.5 2.3 %collective-permute-done.3.p6 = bf16[256,512]{1,0:T(8,128)(2,1)S(1)} collective-permute-done((bf16[256,512]{1,0:T(8,128)(2,1)}, bf16[256,512]{1,0:T(8,128)(2,1)S(1)}, u32[]{:S(2)}, u32[]{:S(2)}) %collective-permute-start.3) | collective-permute-done | bytes 262176 | tf_op jit(solution)/shard_map/ppermute | solution.py:95
  27.8 0.7 broadcast_select_fusion.1
  28.5 2.3 %collective-permute-start.4 = (bf16[256,512]{1,0:T(8,128)(2,1)}, bf16[256,512]{1,0:T(8,128)(2,1)S(1)}, u32[]{:S(2)}, u32[]{:S(2)}) collective-permute-start(bf16[256,512]{1,0:T(8,128)(2,1)} %broadcast_select_fusion.1), channel_id=1, source_target_pairs={{0,4},{2,6},{4,8},{6,10},{8,12},{10,14},{12,0},{14,2},{1,13},{3,15... | collective-permute-start | bytes 786440 | tf_op jit(solution)/shard_map/ppermute | solution.py:107
  30.8 0.0 collective-permute-done.partner
  30.8 0.0 copy-start.10
  30.8 1.9 %collective-permute-start.2 = (bf16[256,512]{1,0:T(8,128)(2,1)S(1)}, bf16[256,512]{1,0:T(8,128)(2,1)S(1)}, u32[]{:S(2)}, u32[]{:S(2)}) collective-permute-start(bf16[256,512]{1,0:T(8,128)(2,1)S(1)} %collective-permute-done.1.p2), channel_id=1, source_target_pairs={{0,14},{2,0},{4,2},{6,4},{8,6},{10,8},{12,10},{14,12},{1,15},{3,1}... | collective-permute-start | bytes 786440 | tf_op jit(solution)/shard_map/ppermute | solution.py:95
  32.8 0.0 collective-permute-done.6.p1
  32.8 3.4 %collective-permute-start.5 = (bf16[256,512]{1,0:T(8,128)(2,1)S(1)}, bf16[256,512]{1,0:T(8,128)(2,1)S(1)}, u32[]{:S(2)}, u32[]{:S(2)}) collective-permute-start(bf16[256,512]{1,0:T(8,128)(2,1)S(1)} %collective-permute-done.3.p6), channel_id=1, source_target_pairs={{0,2},{2,4},{4,6},{6,8},{8,10},{10,12},{12,14},{14,0},{1,3},{3,5},... | collective-permute-start | bytes 786440 | tf_op jit(solution)/shard_map/ppermute | solution.py:95
  36.2 0.0 copy-done.10
  36.2 1.8 %plan.1 = s32[400]{0:T(512)} custom-call(s32[1]{0:T(128)} %bitcast.where, s32[26]{0:T(128)} %copy-done.9, s32[26]{0:T(128)} %copy-done.10), custom_call_target="tpu_custom_call" | custom-call | flops 1000 | bytes 4000 | tf_op jit(solution)/shard_map/plan/pallas_call | solution.py:192
  38.0 0.0 collective-permute-done.7.p7
  38.0 0.0 collective-permute-done.8.other_tiles.tiles
  38.0 0.0 copy-done
  38.0 0.0 copy-start.1
  38.0 1.0 copy-done.1
  39.1 0.9 copy-done.5
  40.0 0.7 copy-done.6
  40.7 1.5 %shard_map.91 = (f32[256,512]{1,0:T(8,128)S(1)}, f32[256,512]{1,0:T(8,128)S(1)}, f32[256,512]{1,0:T(8,128)S(1)}) custom-call(s32[400]{0:T(512)S(1)} %copy-done.6, bf16[256,512]{1,0:T(8,128)(2,1)S(1)} %bitcast.23, bf16[256,512]{1,0:T(8,128)(2,1)S(1)} %collective-permute-done.6.p1, bf16[256,512]{1,0:T(8,128)(2,1)S(1)} %collective-permute-done.1.p2, ...), custom_call_target="tpu_custom_call" | custom-call | flops 536870912 | bytes 3145728 | tf_op jit(solution)/shard_map/pallas_call | solution.py:18
  42.2 0.0 collective-permute-done.4.p4
  42.2 0.1 collective-permute-done.2.p3
  42.3 1.2 collective-permute-done.5.p5
  43.6 0.8 shard_map.93
  44.4 5.2 %collective-permute-start.9 = (f32[256,512]{1,0:T(8,128)S(1)}, f32[256,512]{1,0:T(8,128)S(1)}, u32[]{:S(2)}, u32[]{:S(2)}) collective-permute-start(f32[256,512]{1,0:T(8,128)S(1)} %shard_map.93), channel_id=1, source_target_pairs={{0,1},{1,0},{2,3},{3,2},{4,5},{5,4},{6,7},{7,6},{8,9},{9,8},{10,11... | collective-permute-start | bytes 1572872 | tf_op jit(solution)/shard_map/ppermute | solution.py:99
  49.6 0.0 copy-start.2
  49.6 1.4 shard_map.92.mine
  51.0 0.1 collective-permute-done.9.received
  51.1 0.3 shard_map.94
  51.5 0.0 copy-start.8
  51.5 25.3 %all_to_all.10.hidden = bf16[32,8,512]{2,1,0:T(8,128)(2,1)S(1)} all-to-all(bf16[32,8,512]{2,1,0:T(8,128)(2,1)S(1)} %bitcast.18), channel_id=1, replica_groups=mesh['snap'=32,'vert'=16] {'snap'}, dimensions={0} | all-to-all | bytes 524288 | tf_op jit(solution)/shard_map/all_to_all | solution.py:163
  76.8 0.0 copy-done.8
  76.8 0.6 shard_map.95
  77.4 15.1 %all_to_all.11 = bf16[32,8,512]{2,1,0:T(8,128)(2,1)S(1)} all-to-all(bf16[32,8,512]{2,1,0:T(8,128)(2,1)S(1)} %shard_map.95), channel_id=1, replica_groups=mesh['snap'=32,'vert'=16] {'snap'}, dimensions={0} | all-to-all | bytes 524288 | tf_op jit(solution)/shard_map/all_to_all | solution.py:172
  92.5 2.5 %collective-permute-start.10 = (bf16[256,512]{1,0:T(8,128)(2,1)S(1)}, bf16[256,512]{1,0:T(8,128)(2,1)S(1)}, u32[]{:S(2)}, u32[]{:S(2)}) collective-permute-start(bf16[256,512]{1,0:T(8,128)(2,1)S(1)} %bitcast.13), channel_id=1, source_target_pairs={{0,12},{2,14},{4,0},{6,2},{8,4},{10,6},{12,8},{14,10},{1,13},{3,15... | collective-permute-start | bytes 786440 | tf_op jit(solution)/shard_map/ppermute | solution.py:95
  95.0 3.8 %collective-permute-start.12 = (bf16[256,512]{1,0:T(8,128)(2,1)S(1)}, bf16[256,512]{1,0:T(8,128)(2,1)S(1)}, u32[]{:S(2)}, u32[]{:S(2)}) collective-permute-start(bf16[256,512]{1,0:T(8,128)(2,1)S(1)} %bitcast.14), channel_id=1, source_target_pairs={{0,4},{2,6},{4,8},{6,10},{8,12},{10,14},{12,0},{14,2},{1,5},{3,7},... | collective-permute-start | bytes 786440 | tf_op jit(solution)/shard_map/ppermute | solution.py:95
  98.8 4.3 %collective-permute-start.15 = (bf16[256,512]{1,0:T(8,128)(2,1)S(1)}, bf16[256,512]{1,0:T(8,128)(2,1)S(1)}, u32[]{:S(2)}, u32[]{:S(2)}) collective-permute-start(bf16[256,512]{1,0:T(8,128)(2,1)S(1)} %bitcast.15), channel_id=1, source_target_pairs={{0,14},{2,0},{4,2},{6,4},{8,6},{10,8},{12,10},{14,12},{1,15},{3,1}... | collective-permute-start | bytes 786440 | tf_op jit(solution)/shard_map/ppermute | solution.py:95
  103.1 1.9 %collective-permute-start.16 = (bf16[256,512]{1,0:T(8,128)(2,1)S(1)}, bf16[256,512]{1,0:T(8,128)(2,1)S(1)}, u32[]{:S(2)}, u32[]{:S(2)}) collective-permute-start(bf16[256,512]{1,0:T(8,128)(2,1)S(1)} %bitcast.16), channel_id=1, source_target_pairs={{0,2},{2,4},{4,6},{6,8},{8,10},{10,12},{12,14},{14,0},{1,3},{3,5},... | collective-permute-start | bytes 786440 | tf_op jit(solution)/shard_map/ppermute | solution.py:95
  105.0 0.0 collective-permute-done.10.p2
  105.0 0.9 collective-permute-done.12.p6
  105.9 2.2 %collective-permute-start.13 = (bf16[256,512]{1,0:T(8,128)(2,1)S(1)}, bf16[256,512]{1,0:T(8,128)(2,1)S(1)}, u32[]{:S(2)}, u32[]{:S(2)}) collective-permute-start(bf16[256,512]{1,0:T(8,128)(2,1)S(1)} %broadcast_select_fusion), channel_id=1, source_target_pairs={{0,4},{2,6},{4,8},{6,10},{8,12},{10,14},{12,0},{14,2},{1,13},{3,15... | collective-permute-start | bytes 786440 | tf_op jit(solution)/shard_map/ppermute | solution.py:107
  108.2 8.5 %collective-permute-start.11 = (bf16[256,512]{1,0:T(8,128)(2,1)S(1)}, bf16[256,512]{1,0:T(8,128)(2,1)S(1)}, u32[]{:S(2)}, u32[]{:S(2)}) collective-permute-start(bf16[256,512]{1,0:T(8,128)(2,1)S(1)} %collective-permute-done.10.p2), channel_id=1, source_target_pairs={{0,14},{2,0},{4,2},{6,4},{8,6},{10,8},{12,10},{14,12},{1,15},{3,1}... | collective-permute-start | bytes 786440 | tf_op jit(solution)/shard_map/ppermute | solution.py:95
  116.7 1.9 %collective-permute-start.14 = (bf16[256,512]{1,0:T(8,128)(2,1)S(1)}, bf16[256,512]{1,0:T(8,128)(2,1)S(1)}, u32[]{:S(2)}, u32[]{:S(2)}) collective-permute-start(bf16[256,512]{1,0:T(8,128)(2,1)S(1)} %collective-permute-done.12.p6), channel_id=1, source_target_pairs={{0,2},{2,4},{4,6},{6,8},{8,10},{10,12},{12,14},{14,0},{1,3},{3,5},... | collective-permute-start | bytes 786440 | tf_op jit(solution)/shard_map/ppermute | solution.py:95
  118.6 0.0 collective-permute-done.15.p1
  118.6 0.0 collective-permute-done.16.p7
  118.6 1.5 %shard_map.96 = (f32[256,512]{1,0:T(8,128)S(1)}, f32[256,512]{1,0:T(8,128)S(1)}, f32[256,512]{1,0:T(8,128)S(1)}) custom-call(s32[400]{0:T(512)S(1)} %copy-done.7, bf16[256,512]{1,0:T(8,128)(2,1)S(1)} %bitcast.17, bf16[256,512]{1,0:T(8,128)(2,1)S(1)} %collective-permute-done.15.p1, bf16[256,512]{1,0:T(8,128)(2,1)S(1)} %collective-permute-done.10.p2, ...), custom_call_target="tpu_custom_call" | custom-call | flops 536870912 | bytes 3145728 | tf_op jit(solution)/shard_map/pallas_call | solution.py:18
  120.2 0.0 collective-permute-done.13.p4
  120.2 3.3 %collective-permute-done.11.p3 = bf16[256,512]{1,0:T(8,128)(2,1)S(1)} collective-permute-done((bf16[256,512]{1,0:T(8,128)(2,1)S(1)}, bf16[256,512]{1,0:T(8,128)(2,1)S(1)}, u32[]{:S(2)}, u32[]{:S(2)}) %collective-permute-start.11) | collective-permute-done | bytes 262176 | tf_op jit(solution)/shard_map/ppermute | solution.py:95
  123.4 6.8 %collective-permute-done.14.p5 = bf16[256,512]{1,0:T(8,128)(2,1)S(1)} collective-permute-done((bf16[256,512]{1,0:T(8,128)(2,1)S(1)}, bf16[256,512]{1,0:T(8,128)(2,1)S(1)}, u32[]{:S(2)}, u32[]{:S(2)}) %collective-permute-start.14) | collective-permute-done | bytes 262176 | tf_op jit(solution)/shard_map/ppermute | solution.py:95
  130.3 0.8 shard_map.98
  131.1 5.5 %collective-permute-start.17 = (f32[256,512]{1,0:T(8,128)S(1)}, f32[256,512]{1,0:T(8,128)S(1)}, u32[]{:S(2)}, u32[]{:S(2)}) collective-permute-start(f32[256,512]{1,0:T(8,128)S(1)} %shard_map.98), channel_id=1, source_target_pairs={{0,1},{1,0},{2,3},{3,2},{4,5},{5,4},{6,7},{7,6},{8,9},{9,8},{10,11... | collective-permute-start | bytes 1572872 | tf_op jit(solution)/shard_map/ppermute | solution.py:99
  136.6 0.0 copy-start.4
  136.6 1.4 shard_map.97.mine
  138.0 0.1 collective-permute-done.17.received
  138.1 1.0 shard_map.99
  (11 shorter events, 0.0 us)
Async XLA Ops:
  0.0 38.0 %copy-start = (bf16[1,2,12,128,128]{4,3,2,1,0:T(8,128)(2,1)S(1)}, bf16[1,2,12,128,128]{4,3,2,1,0:T(8,128)(2,1)}, u32[]{:S(2)}) copy-start(bf16[1,2,12,128,128]{4,3,2,1,0:T(8,128)(2,1)} %param.10) | copy-start | bytes 2359300
  0.0 38.0 %collective-permute-start.8 = (bf16[24,128,128]{2,1,0:T(8,128)(2,1)}, bf16[24,128,128]{2,1,0:T(8,128)(2,1)S(1)}, u32[]{:S(2)}, u32[]{:S(2)}) collective-permute-start(bf16[24,128,128]{2,1,0:T(8,128)(2,1)} %bitcast.8), channel_id=1, source_target_pairs={{0,1},{1,0},{2,3},{3,2},{4,5},{5,4},{6,7},{7,6},{8,9},{9,8},{10,11... | collective-permute-start | bytes 2359304 | tf_op jit(solution)/shard_map/ppermute | solution.py:99
  8.9 13.6 %collective-permute-start.1 = (bf16[256,512]{1,0:T(8,128)(2,1)}, bf16[256,512]{1,0:T(8,128)(2,1)S(1)}, u32[]{:S(2)}, u32[]{:S(2)}) collective-permute-start(bf16[256,512]{1,0:T(8,128)(2,1)} %bitcast.19), channel_id=1, source_target_pairs={{0,12},{2,14},{4,0},{6,2},{8,4},{10,6},{12,8},{14,10},{1,13},{3,15... | collective-permute-start | bytes 786440 | tf_op jit(solution)/shard_map/ppermute | solution.py:95
  10.8 17.0 %collective-permute-start.3 = (bf16[256,512]{1,0:T(8,128)(2,1)}, bf16[256,512]{1,0:T(8,128)(2,1)S(1)}, u32[]{:S(2)}, u32[]{:S(2)}) collective-permute-start(bf16[256,512]{1,0:T(8,128)(2,1)} %bitcast.20), channel_id=1, source_target_pairs={{0,4},{2,6},{4,8},{6,10},{8,12},{10,14},{12,0},{14,2},{1,5},{3,7},... | collective-permute-start | bytes 786440 | tf_op jit(solution)/shard_map/ppermute | solution.py:95
  15.1 17.7 %collective-permute-start.6 = (bf16[256,512]{1,0:T(8,128)(2,1)}, bf16[256,512]{1,0:T(8,128)(2,1)S(1)}, u32[]{:S(2)}, u32[]{:S(2)}) collective-permute-start(bf16[256,512]{1,0:T(8,128)(2,1)} %bitcast.21), channel_id=1, source_target_pairs={{0,14},{2,0},{4,2},{6,4},{8,6},{10,8},{12,10},{14,12},{1,15},{3,1}... | collective-permute-start | bytes 786440 | tf_op jit(solution)/shard_map/ppermute | solution.py:95
  17.0 21.0 %collective-permute-start.7 = (bf16[256,512]{1,0:T(8,128)(2,1)}, bf16[256,512]{1,0:T(8,128)(2,1)S(1)}, u32[]{:S(2)}, u32[]{:S(2)}) collective-permute-start(bf16[256,512]{1,0:T(8,128)(2,1)} %bitcast.22), channel_id=1, source_target_pairs={{0,2},{2,4},{4,6},{6,8},{8,10},{10,12},{12,14},{14,0},{1,3},{3,5},... | collective-permute-start | bytes 786440 | tf_op jit(solution)/shard_map/ppermute | solution.py:95
  22.0 0.5 copy-start.9
  22.5 8.3 %collective-permute-start = (s32[26]{0:T(128)S(1)}, s32[26]{0:T(128)S(1)}, u32[]{:S(2)}, u32[]{:S(2)}) collective-permute-start(s32[26]{0:T(128)S(1)} %reshape.13.own), channel_id=1, source_target_pairs={{0,1},{1,0},{2,3},{3,2},{4,5},{5,4},{6,7},{7,6},{8,9},{9,8},{10,11... | collective-permute-start | bytes 320 | tf_op jit(solution)/shard_map/ppermute | solution.py:99
  28.5 13.7 %collective-permute-start.4 = (bf16[256,512]{1,0:T(8,128)(2,1)}, bf16[256,512]{1,0:T(8,128)(2,1)S(1)}, u32[]{:S(2)}, u32[]{:S(2)}) collective-permute-start(bf16[256,512]{1,0:T(8,128)(2,1)} %broadcast_select_fusion.1), channel_id=1, source_target_pairs={{0,4},{2,6},{4,8},{6,10},{8,12},{10,14},{12,0},{14,2},{1,13},{3,15... | collective-permute-start | bytes 786440 | tf_op jit(solution)/shard_map/ppermute | solution.py:107
  30.8 5.3 %copy-start.10 = (s32[26]{0:T(128)}, s32[26]{0:T(128)S(1)}, u32[]{:S(2)}) copy-start(s32[26]{0:T(128)S(1)} %collective-permute-done.partner) | copy-start | bytes 316
  30.8 11.5 %collective-permute-start.2 = (bf16[256,512]{1,0:T(8,128)(2,1)S(1)}, bf16[256,512]{1,0:T(8,128)(2,1)S(1)}, u32[]{:S(2)}, u32[]{:S(2)}) collective-permute-start(bf16[256,512]{1,0:T(8,128)(2,1)S(1)} %collective-permute-done.1.p2), channel_id=1, source_target_pairs={{0,14},{2,0},{4,2},{6,4},{8,6},{10,8},{12,10},{14,12},{1,15},{3,1}... | collective-permute-start | bytes 786440 | tf_op jit(solution)/shard_map/ppermute | solution.py:95
  32.8 10.8 %collective-permute-start.5 = (bf16[256,512]{1,0:T(8,128)(2,1)S(1)}, bf16[256,512]{1,0:T(8,128)(2,1)S(1)}, u32[]{:S(2)}, u32[]{:S(2)}) collective-permute-start(bf16[256,512]{1,0:T(8,128)(2,1)S(1)} %collective-permute-done.3.p6), channel_id=1, source_target_pairs={{0,2},{2,4},{4,6},{6,8},{8,10},{10,12},{12,14},{14,0},{1,3},{3,5},... | collective-permute-start | bytes 786440 | tf_op jit(solution)/shard_map/ppermute | solution.py:95
  38.0 1.0 copy-start.1
  39.1 0.9 copy-start.5
  40.0 0.7 copy-start.6
  44.4 6.7 %collective-permute-start.9 = (f32[256,512]{1,0:T(8,128)S(1)}, f32[256,512]{1,0:T(8,128)S(1)}, u32[]{:S(2)}, u32[]{:S(2)}) collective-permute-start(f32[256,512]{1,0:T(8,128)S(1)} %shard_map.93), channel_id=1, source_target_pairs={{0,1},{1,0},{2,3},{3,2},{4,5},{5,4},{6,7},{7,6},{8,9},{9,8},{10,11... | collective-permute-start | bytes 1572872 | tf_op jit(solution)/shard_map/ppermute | solution.py:99
  49.6 1.5 %copy-start.2 = (bf16[512,512]{1,0:T(8,128)(2,1)S(1)}, bf16[512,512]{1,0:T(8,128)(2,1)}, u32[]{:S(2)}) copy-start(bf16[512,512]{1,0:T(8,128)(2,1)} %w_message.2) | copy-start | bytes 1572868
  51.5 25.3 %copy-start.8 = (f32[16,512]{1,0:T(8,128)S(1)}, f32[16,512]{1,0:T(8,128)}, u32[]{:S(2)}) copy-start(f32[16,512]{1,0:T(8,128)} %taps.1) | copy-start | bytes 98308
  92.5 26.2 %copy-start.3 = (bf16[512,512]{1,0:T(8,128)(2,1)S(1)}, bf16[512,512]{1,0:T(8,128)(2,1)}, u32[]{:S(2)}) copy-start(bf16[512,512]{1,0:T(8,128)(2,1)} %w_root.3) | copy-start | bytes 1572868
  92.5 26.2 %copy-start.7 = (s32[400]{0:T(512)S(1)}, s32[400]{0:T(512)}, u32[]{:S(2)}) copy-start(s32[400]{0:T(512)} %plan.1) | copy-start | bytes 4804
  92.5 12.5 %collective-permute-start.10 = (bf16[256,512]{1,0:T(8,128)(2,1)S(1)}, bf16[256,512]{1,0:T(8,128)(2,1)S(1)}, u32[]{:S(2)}, u32[]{:S(2)}) collective-permute-start(bf16[256,512]{1,0:T(8,128)(2,1)S(1)} %bitcast.13), channel_id=1, source_target_pairs={{0,12},{2,14},{4,0},{6,2},{8,4},{10,6},{12,8},{14,10},{1,13},{3,15... | collective-permute-start | bytes 786440 | tf_op jit(solution)/shard_map/ppermute | solution.py:95
  95.0 10.9 %collective-permute-start.12 = (bf16[256,512]{1,0:T(8,128)(2,1)S(1)}, bf16[256,512]{1,0:T(8,128)(2,1)S(1)}, u32[]{:S(2)}, u32[]{:S(2)}) collective-permute-start(bf16[256,512]{1,0:T(8,128)(2,1)S(1)} %bitcast.14), channel_id=1, source_target_pairs={{0,4},{2,6},{4,8},{6,10},{8,12},{10,14},{12,0},{14,2},{1,5},{3,7},... | collective-permute-start | bytes 786440 | tf_op jit(solution)/shard_map/ppermute | solution.py:95
  98.8 19.8 %collective-permute-start.15 = (bf16[256,512]{1,0:T(8,128)(2,1)S(1)}, bf16[256,512]{1,0:T(8,128)(2,1)S(1)}, u32[]{:S(2)}, u32[]{:S(2)}) collective-permute-start(bf16[256,512]{1,0:T(8,128)(2,1)S(1)} %bitcast.15), channel_id=1, source_target_pairs={{0,14},{2,0},{4,2},{6,4},{8,6},{10,8},{12,10},{14,12},{1,15},{3,1}... | collective-permute-start | bytes 786440 | tf_op jit(solution)/shard_map/ppermute | solution.py:95
  103.1 15.5 %collective-permute-start.16 = (bf16[256,512]{1,0:T(8,128)(2,1)S(1)}, bf16[256,512]{1,0:T(8,128)(2,1)S(1)}, u32[]{:S(2)}, u32[]{:S(2)}) collective-permute-start(bf16[256,512]{1,0:T(8,128)(2,1)S(1)} %bitcast.16), channel_id=1, source_target_pairs={{0,2},{2,4},{4,6},{6,8},{8,10},{10,12},{12,14},{14,0},{1,3},{3,5},... | collective-permute-start | bytes 786440 | tf_op jit(solution)/shard_map/ppermute | solution.py:95
  105.9 14.2 %collective-permute-start.13 = (bf16[256,512]{1,0:T(8,128)(2,1)S(1)}, bf16[256,512]{1,0:T(8,128)(2,1)S(1)}, u32[]{:S(2)}, u32[]{:S(2)}) collective-permute-start(bf16[256,512]{1,0:T(8,128)(2,1)S(1)} %broadcast_select_fusion), channel_id=1, source_target_pairs={{0,4},{2,6},{4,8},{6,10},{8,12},{10,14},{12,0},{14,2},{1,13},{3,15... | collective-permute-start | bytes 786440 | tf_op jit(solution)/shard_map/ppermute | solution.py:107
  108.2 15.3 %collective-permute-start.11 = (bf16[256,512]{1,0:T(8,128)(2,1)S(1)}, bf16[256,512]{1,0:T(8,128)(2,1)S(1)}, u32[]{:S(2)}, u32[]{:S(2)}) collective-permute-start(bf16[256,512]{1,0:T(8,128)(2,1)S(1)} %collective-permute-done.10.p2), channel_id=1, source_target_pairs={{0,14},{2,0},{4,2},{6,4},{8,6},{10,8},{12,10},{14,12},{1,15},{3,1}... | collective-permute-start | bytes 786440 | tf_op jit(solution)/shard_map/ppermute | solution.py:95
  116.7 13.6 %collective-permute-start.14 = (bf16[256,512]{1,0:T(8,128)(2,1)S(1)}, bf16[256,512]{1,0:T(8,128)(2,1)S(1)}, u32[]{:S(2)}, u32[]{:S(2)}) collective-permute-start(bf16[256,512]{1,0:T(8,128)(2,1)S(1)} %collective-permute-done.12.p6), channel_id=1, source_target_pairs={{0,2},{2,4},{4,6},{6,8},{8,10},{10,12},{12,14},{14,0},{1,3},{3,5},... | collective-permute-start | bytes 786440 | tf_op jit(solution)/shard_map/ppermute | solution.py:95
  131.1 7.0 %collective-permute-start.17 = (f32[256,512]{1,0:T(8,128)S(1)}, f32[256,512]{1,0:T(8,128)S(1)}, u32[]{:S(2)}, u32[]{:S(2)}) collective-permute-start(f32[256,512]{1,0:T(8,128)S(1)} %shard_map.98), channel_id=1, source_target_pairs={{0,1},{1,0},{2,3},{3,2},{4,5},{5,4},{6,7},{7,6},{8,9},{9,8},{10,11... | collective-permute-start | bytes 1572872 | tf_op jit(solution)/shard_map/ppermute | solution.py:99
  136.6 1.5 %copy-start.4 = (bf16[512,512]{1,0:T(8,128)(2,1)S(1)}, bf16[512,512]{1,0:T(8,128)(2,1)}, u32[]{:S(2)}) copy-start(bf16[512,512]{1,0:T(8,128)(2,1)} %w_message.3) | copy-start | bytes 1572868
where the time goes:
time: 140 us; the launch traced here: 139 us
  starting transfers between devices  66.8 us (48%)
  blocking collectives  40.4 us (29%)
  waiting for transfers between devices  15.5 us (11%)
  Pallas kernels  11.2 us (8%)
  local copies, waits for them, and re-layouts  3.52 us (3%)
  other arithmetic  1.51 us (1%)
    ppermute x12, starting transfers between devices, shift(): return lax.ppermute(x, 'vert', moves(distance, distance))  39.7 us
    all_to_all x1, blocking collectives, temporal(): by_vertex = lax.all_to_all(split, 'snap', split_axis=0, concat_axis=0)  25.3 us
    ppermute x4, starting transfers between devices, swap(): return lax.ppermute(x, 'vert', [(v, v ^ 1) for v in range(2 * RING)])  22.6 us
    ppermute x12, waiting for transfers between devices, shift(): return lax.ppermute(x, 'vert', moves(distance, distance))  15.2 us
    all_to_all x1, blocking collectives, temporal(): returned = lax.all_to_all(mixed, 'snap', split_axis=0, concat_axis=0)  15.1 us
    pallas_call x9, Pallas kernels, call(): pl.pallas_call(kernel, out_shape=outs, in_specs=specs, out_specs=jax.tree...  9.38 us
    ppermute x2, starting transfers between devices, ring_gather(): across = lax.ppermute(jnp.where(first, up2, down2), 'vert', moves(2, -2))  4.51 us
  transfers between devices with their start and end apart: 18, of which 9 were waited for; matrix products, arithmetic and copies ran while one was open for 2% of the time, Pallas kernels for 5%

commit v1 on v0

--- a/solution.py
+++ b/solution.py
@@ -38,7 +38,8 @@
             @pl.loop(0, table[r * (slots + 1) + slots])
             def _(k):
                 column = table[r * (slots + 1) + k]
-                near = lax.rem(column // 4 - y + RING, RING) * 2 + side
+                step = (column // 4 - y) * (1 - 2 * core)
+                near = lax.rem(step + RING, RING) * 2 + side
 
                 @pl.when(lax.rem(column // 2, 2) == core)
                 def _():
@@ -85,14 +86,11 @@
     out[...] = jnp.maximum(full, 0.0).astype(jnp.bfloat16)
 
 
-def moves(up, down):
-    return [(2 * y, (2 * y + 2 * up) % (2 * RING)) for y in range(RING)] + [
-        (2 * y + 1, (2 * y + 2 * down) % (2 * RING) + 1) for y in range(RING)
-    ]
-
-
 def shift(x, distance):
-    return lax.ppermute(x, "vert", moves(distance, distance))
+    chips = range(RING)
+    pairs = [(2 * y, (2 * y + 2 * distance) % (2 * RING)) for y in chips]
+    pairs += [(2 * y + 1, (2 * y - 2 * distance) % (2 * RING) + 1) for y in chips]
+    return lax.ppermute(x, "vert", pairs)
 
 
 def swap(x):
@@ -100,12 +98,11 @@
 
 
 def ring_gather(own):
-    first = lax.rem(lax.axis_index("vert"), 2) == 0
-    up2, down2 = shift(own, 2), shift(own, -2)
-    up1, down1 = shift(own, 1), shift(own, -1)
-    up3, down3 = shift(up2, 1), shift(down2, -1)
-    across = lax.ppermute(jnp.where(first, up2, down2), "vert", moves(2, -2))
-    return (own, down1, down2, down3, across, up3, up2, up1)
+    ahead2, back2 = shift(own, 2), shift(own, -2)
+    ahead1, back1 = shift(own, 1), shift(own, -1)
+    across = shift(ahead2, 2)
+    ahead3, back3 = shift(ahead2, 1), shift(back2, -1)
+    return (own, back1, back2, back3, across, ahead3, ahead2, ahead1)
 
 
 def graph_layer(pieces, own_tiles, other_tiles, plan, w_message, w_root):

time: 140 us -> 134 us (0.957)
  starting transfers between devices: 66.8 us -> 62.4 us
  blocking collectives: 40.4 us -> 37 us
  other arithmetic: 1.51 us -> 0.07 us
    all_to_all x1, blocking collectives: 25.3 us -> 21.9 us  [temporal(): by_vertex = lax.all_to_all(split, 'snap', split_axis=0, concat_axis=0)]
    ppermute x14, starting transfers between devices: 44.2 us -> 40.8 us  [shift(): return lax.ppermute(x, 'vert', pairs)]
    unnamed x22 -> x28, local copies, waits for them, and re-layouts: 2.69 us -> 4.52 us
  transfers between devices with their start and end apart: 18 -> 18, of which waited for: 9 -> 8; matrix products, arithmetic and copies ran while one was open for 2% -> 0% of each run, Pallas kernels for 5% -> 6%
where the time goes in v1:
time: 134 us; the launch traced here: 133 us
  starting transfers between devices  62.4 us (47%)
  blocking collectives  37 us (28%)
  waiting for transfers between devices  16.9 us (13%)
  Pallas kernels  11.2 us (8%)
  local copies, waits for them, and re-layouts  4.7 us (4%)
    ppermute x14, starting transfers between devices, shift(): return lax.ppermute(x, 'vert', pairs)  40.8 us
    all_to_all x1, blocking collectives, temporal(): by_vertex = lax.all_to_all(split, 'snap', split_axis=0, concat_axis=0)  21.9 us
    ppermute x4, starting transfers between devices, swap(): return lax.ppermute(x, 'vert', [(v, v ^ 1) for v in range(2 * RING)])  21.6 us
    ppermute x14, waiting for transfers between devices, shift(): return lax.ppermute(x, 'vert', pairs)  15.9 us
    all_to_all x1, blocking collectives, temporal(): returned = lax.all_to_all(mixed, 'snap', split_axis=0, concat_axis=0)  15.1 us
    pallas_call x9, Pallas kernels, call(): pl.pallas_call(kernel, out_shape=outs, in_specs=specs, out_specs=jax.tree...  9.36 us
    unnamed x28, local copies, waits for them, and re-layouts  4.52 us
  transfers between devices with their start and end apart: 18, of which 8 were waited for; matrix products, arithmetic and copies ran while one was open for 0% of the time, Pallas kernels for 6%

profile of v1, /device:TPU:1, one launch (start us, length us, event | category | flops | bytes accessed | tf_op | source)
XLA Modules:
  0.0 132.6 jit_solution(11107380032672945019)
XLA Ops:
  0.0 8.7 %collective-permute-start.8 = (bf16[24,128,128]{2,1,0:T(8,128)(2,1)}, bf16[24,128,128]{2,1,0:T(8,128)(2,1)S(1)}, u32[]{:S(2)}, u32[]{:S(2)}) collective-permute-start(bf16[24,128,128]{2,1,0:T(8,128)(2,1)} %bitcast.8), channel_id=1, source_target_pairs={{0,1},{1,0},{2,3},{3,2},{4,5},{5,4},{6,7},{7,6},{8,9},{9,8},{10,11... | collective-permute-start | bytes 2359304 | tf_op jit(solution)/shard_map/ppermute | solution.py:97
  8.7 0.0 copy-start.13
  8.8 1.9 %collective-permute-start.3 = (bf16[256,512]{1,0:T(8,128)(2,1)}, bf16[256,512]{1,0:T(8,128)(2,1)S(1)}, u32[]{:S(2)}, u32[]{:S(2)}) collective-permute-start(bf16[256,512]{1,0:T(8,128)(2,1)} %bitcast.19), channel_id=1, source_target_pairs={{0,4},{2,6},{4,8},{6,10},{8,12},{10,14},{12,0},{14,2},{1,13},{3,15... | collective-permute-start | bytes 786440 | tf_op jit(solution)/shard_map/ppermute | solution.py:93
  10.7 4.3 %collective-permute-start.1 = (bf16[256,512]{1,0:T(8,128)(2,1)}, bf16[256,512]{1,0:T(8,128)(2,1)S(1)}, u32[]{:S(2)}, u32[]{:S(2)}) collective-permute-start(bf16[256,512]{1,0:T(8,128)(2,1)} %bitcast.20), channel_id=1, source_target_pairs={{0,12},{2,14},{4,0},{6,2},{8,4},{10,6},{12,8},{14,10},{1,5},{3,7},... | collective-permute-start | bytes 786440 | tf_op jit(solution)/shard_map/ppermute | solution.py:93
  15.0 1.9 %collective-permute-start.6 = (bf16[256,512]{1,0:T(8,128)(2,1)}, bf16[256,512]{1,0:T(8,128)(2,1)S(1)}, u32[]{:S(2)}, u32[]{:S(2)}) collective-permute-start(bf16[256,512]{1,0:T(8,128)(2,1)} %bitcast.21), channel_id=1, source_target_pairs={{0,14},{2,0},{4,2},{6,4},{8,6},{10,8},{12,10},{14,12},{1,3},{3,5},... | collective-permute-start | bytes 786440 | tf_op jit(solution)/shard_map/ppermute | solution.py:93
  16.9 0.1 copy.14
  17.0 0.7 copy-done.10
  17.7 0.1 pad_add_fusion
  17.7 0.1 reshape.13.own
  17.8 3.7 %collective-permute-start = (s32[26]{0:T(128)S(1)}, s32[26]{0:T(128)S(1)}, u32[]{:S(2)}, u32[]{:S(2)}) collective-permute-start(s32[26]{0:T(128)S(1)} %reshape.13.own), channel_id=1, source_target_pairs={{0,1},{1,0},{2,3},{3,2},{4,5},{5,4},{6,7},{7,6},{8,9},{9,8},{10,11... | collective-permute-start | bytes 320 | tf_op jit(solution)/shard_map/ppermute | solution.py:97
  21.5 0.8 collective-permute-done.partner
  22.3 3.1 %collective-permute-start.7 = (bf16[256,512]{1,0:T(8,128)(2,1)}, bf16[256,512]{1,0:T(8,128)(2,1)S(1)}, u32[]{:S(2)}, u32[]{:S(2)}) collective-permute-start(bf16[256,512]{1,0:T(8,128)(2,1)} %bitcast.22), channel_id=1, source_target_pairs={{0,2},{2,4},{4,6},{6,8},{8,10},{10,12},{12,14},{14,0},{1,15},{3,1}... | collective-permute-start | bytes 786440 | tf_op jit(solution)/shard_map/ppermute | solution.py:93
  25.4 0.0 collective-permute-done.3.p6
  25.5 1.9 %collective-permute-start.4 = (bf16[256,512]{1,0:T(8,128)(2,1)S(1)}, bf16[256,512]{1,0:T(8,128)(2,1)S(1)}, u32[]{:S(2)}, u32[]{:S(2)}) collective-permute-start(bf16[256,512]{1,0:T(8,128)(2,1)S(1)} %collective-permute-done.3.p6), channel_id=1, source_target_pairs={{0,4},{2,6},{4,8},{6,10},{8,12},{10,14},{12,0},{14,2},{1,13},{3,15... | collective-permute-start | bytes 786440 | tf_op jit(solution)/shard_map/ppermute | solution.py:93
  27.4 0.0 collective-permute-done.1.p2
  27.4 1.9 %collective-permute-start.5 = (bf16[256,512]{1,0:T(8,128)(2,1)S(1)}, bf16[256,512]{1,0:T(8,128)(2,1)S(1)}, u32[]{:S(2)}, u32[]{:S(2)}) collective-permute-start(bf16[256,512]{1,0:T(8,128)(2,1)S(1)} %collective-permute-done.3.p6), channel_id=1, source_target_pairs={{0,2},{2,4},{4,6},{6,8},{8,10},{10,12},{12,14},{14,0},{1,15},{3,1}... | collective-permute-start | bytes 786440 | tf_op jit(solution)/shard_map/ppermute | solution.py:93
  29.3 0.0 collective-permute-done.6.p1
  29.3 3.4 %collective-permute-start.2 = (bf16[256,512]{1,0:T(8,128)(2,1)S(1)}, bf16[256,512]{1,0:T(8,128)(2,1)S(1)}, u32[]{:S(2)}, u32[]{:S(2)}) collective-permute-start(bf16[256,512]{1,0:T(8,128)(2,1)S(1)} %collective-permute-done.1.p2), channel_id=1, source_target_pairs={{0,14},{2,0},{4,2},{6,4},{8,6},{10,8},{12,10},{14,12},{1,3},{3,5},... | collective-permute-start | bytes 786440 | tf_op jit(solution)/shard_map/ppermute | solution.py:93
  32.7 0.0 copy-done.11
  32.7 0.0 copy-done.12
  32.7 1.8 %plan.1 = s32[400]{0:T(512)} custom-call(s32[1]{0:T(128)} %bitcast.where, s32[26]{0:T(128)} %copy-done.11, s32[26]{0:T(128)} %copy-done.12), custom_call_target="tpu_custom_call" | custom-call | flops 1000 | bytes 4000 | tf_op jit(solution)/shard_map/plan/pallas_call | solution.py:189
  34.5 0.0 collective-permute-done.7.p7
  34.5 0.0 collective-permute-done.8.other_tiles.tiles
  34.6 0.0 copy-start
  34.6 1.1 copy-done
  35.7 1.0 copy-done.2
  36.7 0.9 copy-done.6
  37.7 0.7 copy-done.7
  38.4 1.5 %shard_map.91 = (f32[256,512]{1,0:T(8,128)S(1)}, f32[256,512]{1,0:T(8,128)S(1)}, f32[256,512]{1,0:T(8,128)S(1)}) custom-call(s32[400]{0:T(512)S(1)} %copy-done.7, bf16[256,512]{1,0:T(8,128)(2,1)S(1)} %bitcast.23, bf16[256,512]{1,0:T(8,128)(2,1)S(1)} %collective-permute-done.6.p1, bf16[256,512]{1,0:T(8,128)(2,1)S(1)} %collective-permute-done.1.p2, ...), custom_call_target="tpu_custom_call" | custom-call | flops 536870912 | bytes 3145728 | tf_op jit(solution)/shard_map/pallas_call | solution.py:18
  39.9 0.0 collective-permute-done.4.p4
  39.9 0.4 collective-permute-done.5.p5
  40.3 2.3 %collective-permute-done.2.p3 = bf16[256,512]{1,0:T(8,128)(2,1)S(1)} collective-permute-done((bf16[256,512]{1,0:T(8,128)(2,1)S(1)}, bf16[256,512]{1,0:T(8,128)(2,1)S(1)}, u32[]{:S(2)}, u32[]{:S(2)}) %collective-permute-start.2) | collective-permute-done | bytes 262176 | tf_op jit(solution)/shard_map/ppermute | solution.py:93
  42.5 0.8 shard_map.93
  43.4 4.0 %collective-permute-start.9 = (f32[256,512]{1,0:T(8,128)S(1)}, f32[256,512]{1,0:T(8,128)S(1)}, u32[]{:S(2)}, u32[]{:S(2)}) collective-permute-start(f32[256,512]{1,0:T(8,128)S(1)} %shard_map.93), channel_id=1, source_target_pairs={{0,1},{1,0},{2,3},{3,2},{4,5},{5,4},{6,7},{7,6},{8,9},{9,8},{10,11... | collective-permute-start | bytes 1572872 | tf_op jit(solution)/shard_map/ppermute | solution.py:97
  47.4 0.0 copy-start.3
  47.4 1.4 %shard_map.92.mine = f32[256,512]{1,0:T(8,128)S(1)} custom-call(s32[400]{0:T(512)S(1)} %copy-done.7, bf16[256,512]{1,0:T(8,128)(2,1)S(1)} %collective-permute-done.2.p3, bf16[256,512]{1,0:T(8,128)(2,1)S(1)} %collective-permute-done.4.p4, bf16[256,512]{1,0:T(8,128)(2,1)S(1)} %collective-permute-done.5.p5, ...), custom_call_target="tpu_custom_call", output_to_operand_aliasing={{}: (5, {})} | custom-call | flops 134217728 | bytes 1048576 | tf_op jit(solution)/shard_map/pallas_call | solution.py:18
  48.8 0.1 collective-permute-done.9.received
  48.9 0.3 shard_map.94
  49.3 0.0 copy-start.9
  49.3 21.9 %all_to_all.10.hidden = bf16[32,8,512]{2,1,0:T(8,128)(2,1)S(1)} all-to-all(bf16[32,8,512]{2,1,0:T(8,128)(2,1)S(1)} %bitcast.18), channel_id=1, replica_groups=mesh['snap'=32,'vert'=16] {'snap'}, dimensions={0} | all-to-all | bytes 524288 | tf_op jit(solution)/shard_map/all_to_all | solution.py:160
  71.2 0.6 shard_map.95
  71.8 0.0 copy-start.8
  71.8 15.1 %all_to_all.11 = bf16[32,8,512]{2,1,0:T(8,128)(2,1)S(1)} all-to-all(bf16[32,8,512]{2,1,0:T(8,128)(2,1)S(1)} %shard_map.95), channel_id=1, replica_groups=mesh['snap'=32,'vert'=16] {'snap'}, dimensions={0} | all-to-all | bytes 524288 | tf_op jit(solution)/shard_map/all_to_all | solution.py:169
  86.9 4.1 %collective-permute-start.10 = (bf16[256,512]{1,0:T(8,128)(2,1)S(1)}, bf16[256,512]{1,0:T(8,128)(2,1)S(1)}, u32[]{:S(2)}, u32[]{:S(2)}) collective-permute-start(bf16[256,512]{1,0:T(8,128)(2,1)S(1)} %bitcast.13), channel_id=1, source_target_pairs={{0,12},{2,14},{4,0},{6,2},{8,4},{10,6},{12,8},{14,10},{1,5},{3,7},... | collective-permute-start | bytes 786440 | tf_op jit(solution)/shard_map/ppermute | solution.py:93
  91.0 3.3 %collective-permute-start.12 = (bf16[256,512]{1,0:T(8,128)(2,1)S(1)}, bf16[256,512]{1,0:T(8,128)(2,1)S(1)}, u32[]{:S(2)}, u32[]{:S(2)}) collective-permute-start(bf16[256,512]{1,0:T(8,128)(2,1)S(1)} %bitcast.14), channel_id=1, source_target_pairs={{0,4},{2,6},{4,8},{6,10},{8,12},{10,14},{12,0},{14,2},{1,13},{3,15... | collective-permute-start | bytes 786440 | tf_op jit(solution)/shard_map/ppermute | solution.py:93
  94.3 2.4 %collective-permute-start.15 = (bf16[256,512]{1,0:T(8,128)(2,1)S(1)}, bf16[256,512]{1,0:T(8,128)(2,1)S(1)}, u32[]{:S(2)}, u32[]{:S(2)}) collective-permute-start(bf16[256,512]{1,0:T(8,128)(2,1)S(1)} %bitcast.15), channel_id=1, source_target_pairs={{0,14},{2,0},{4,2},{6,4},{8,6},{10,8},{12,10},{14,12},{1,3},{3,5},... | collective-permute-start | bytes 786440 | tf_op jit(solution)/shard_map/ppermute | solution.py:93
  96.7 4.1 %collective-permute-start.16 = (bf16[256,512]{1,0:T(8,128)(2,1)S(1)}, bf16[256,512]{1,0:T(8,128)(2,1)S(1)}, u32[]{:S(2)}, u32[]{:S(2)}) collective-permute-start(bf16[256,512]{1,0:T(8,128)(2,1)S(1)} %bitcast.16), channel_id=1, source_target_pairs={{0,2},{2,4},{4,6},{6,8},{8,10},{10,12},{12,14},{14,0},{1,15},{3,1}... | collective-permute-start | bytes 786440 | tf_op jit(solution)/shard_map/ppermute | solution.py:93
  100.8 0.0 collective-permute-done.10.p2
  100.8 1.9 %collective-permute-start.11 = (bf16[256,512]{1,0:T(8,128)(2,1)S(1)}, bf16[256,512]{1,0:T(8,128)(2,1)S(1)}, u32[]{:S(2)}, u32[]{:S(2)}) collective-permute-start(bf16[256,512]{1,0:T(8,128)(2,1)S(1)} %collective-permute-done.10.p2), channel_id=1, source_target_pairs={{0,14},{2,0},{4,2},{6,4},{8,6},{10,8},{12,10},{14,12},{1,3},{3,5},... | collective-permute-start | bytes 786440 | tf_op jit(solution)/shard_map/ppermute | solution.py:93
  102.7 4.4 %collective-permute-done.12.p6 = bf16[256,512]{1,0:T(8,128)(2,1)S(1)} collective-permute-done((bf16[256,512]{1,0:T(8,128)(2,1)S(1)}, bf16[256,512]{1,0:T(8,128)(2,1)S(1)}, u32[]{:S(2)}, u32[]{:S(2)}) %collective-permute-start.12) | collective-permute-done | bytes 262176 | tf_op jit(solution)/shard_map/ppermute | solution.py:93
  107.1 4.6 %collective-permute-start.13 = (bf16[256,512]{1,0:T(8,128)(2,1)S(1)}, bf16[256,512]{1,0:T(8,128)(2,1)S(1)}, u32[]{:S(2)}, u32[]{:S(2)}) collective-permute-start(bf16[256,512]{1,0:T(8,128)(2,1)S(1)} %collective-permute-done.12.p6), channel_id=1, source_target_pairs={{0,4},{2,6},{4,8},{6,10},{8,12},{10,14},{12,0},{14,2},{1,13},{3,15... | collective-permute-start | bytes 786440 | tf_op jit(solution)/shard_map/ppermute | solution.py:93
  111.8 1.9 %collective-permute-start.14 = (bf16[256,512]{1,0:T(8,128)(2,1)S(1)}, bf16[256,512]{1,0:T(8,128)(2,1)S(1)}, u32[]{:S(2)}, u32[]{:S(2)}) collective-permute-start(bf16[256,512]{1,0:T(8,128)(2,1)S(1)} %collective-permute-done.12.p6), channel_id=1, source_target_pairs={{0,2},{2,4},{4,6},{6,8},{8,10},{10,12},{12,14},{14,0},{1,15},{3,1}... | collective-permute-start | bytes 786440 | tf_op jit(solution)/shard_map/ppermute | solution.py:93
  113.7 0.0 collective-permute-done.15.p1
  113.7 0.0 collective-permute-done.16.p7
  113.7 1.5 %shard_map.96 = (f32[256,512]{1,0:T(8,128)S(1)}, f32[256,512]{1,0:T(8,128)S(1)}, f32[256,512]{1,0:T(8,128)S(1)}) custom-call(s32[400]{0:T(512)S(1)} %copy-done.8, bf16[256,512]{1,0:T(8,128)(2,1)S(1)} %bitcast.17, bf16[256,512]{1,0:T(8,128)(2,1)S(1)} %collective-permute-done.15.p1, bf16[256,512]{1,0:T(8,128)(2,1)S(1)} %collective-permute-done.10.p2, ...), custom_call_target="tpu_custom_call" | custom-call | flops 536870912 | bytes 3145728 | tf_op jit(solution)/shard_map/pallas_call | solution.py:18
  115.3 0.0 collective-permute-done.11.p3
  115.3 5.6 %collective-permute-done.13.p4 = bf16[256,512]{1,0:T(8,128)(2,1)S(1)} collective-permute-done((bf16[256,512]{1,0:T(8,128)(2,1)S(1)}, bf16[256,512]{1,0:T(8,128)(2,1)S(1)}, u32[]{:S(2)}, u32[]{:S(2)}) %collective-permute-start.13) | collective-permute-done | bytes 262176 | tf_op jit(solution)/shard_map/ppermute | solution.py:93
  120.9 3.2 %collective-permute-done.14.p5 = bf16[256,512]{1,0:T(8,128)(2,1)S(1)} collective-permute-done((bf16[256,512]{1,0:T(8,128)(2,1)S(1)}, bf16[256,512]{1,0:T(8,128)(2,1)S(1)}, u32[]{:S(2)}, u32[]{:S(2)}) %collective-permute-start.14) | collective-permute-done | bytes 262176 | tf_op jit(solution)/shard_map/ppermute | solution.py:93
  124.1 0.8 shard_map.98
  124.9 5.2 %collective-permute-start.17 = (f32[256,512]{1,0:T(8,128)S(1)}, f32[256,512]{1,0:T(8,128)S(1)}, u32[]{:S(2)}, u32[]{:S(2)}) collective-permute-start(f32[256,512]{1,0:T(8,128)S(1)} %shard_map.98), channel_id=1, source_target_pairs={{0,1},{1,0},{2,3},{3,2},{4,5},{5,4},{6,7},{7,6},{8,9},{9,8},{10,11... | collective-permute-start | bytes 1572872 | tf_op jit(solution)/shard_map/ppermute | solution.py:97
  130.1 0.0 copy-start.5
  130.1 1.4 %shard_map.97.mine = f32[256,512]{1,0:T(8,128)S(1)} custom-call(s32[400]{0:T(512)S(1)} %copy-done.8, bf16[256,512]{1,0:T(8,128)(2,1)S(1)} %collective-permute-done.11.p3, bf16[256,512]{1,0:T(8,128)(2,1)S(1)} %collective-permute-done.13.p4, bf16[256,512]{1,0:T(8,128)(2,1)S(1)} %collective-permute-done.14.p5, ...), custom_call_target="tpu_custom_call", output_to_operand_aliasing={{}: (5, {})} | custom-call | flops 134217728 | bytes 1048576 | tf_op jit(solution)/shard_map/pallas_call | solution.py:18
  131.5 0.1 collective-permute-done.17.received
  131.6 1.0 shard_map.99
  (15 shorter events, 0.0 us)
Async XLA Ops:
  0.0 34.5 %collective-permute-start.8 = (bf16[24,128,128]{2,1,0:T(8,128)(2,1)}, bf16[24,128,128]{2,1,0:T(8,128)(2,1)S(1)}, u32[]{:S(2)}, u32[]{:S(2)}) collective-permute-start(bf16[24,128,128]{2,1,0:T(8,128)(2,1)} %bitcast.8), channel_id=1, source_target_pairs={{0,1},{1,0},{2,3},{3,2},{4,5},{5,4},{6,7},{7,6},{8,9},{9,8},{10,11... | collective-permute-start | bytes 2359304 | tf_op jit(solution)/shard_map/ppermute | solution.py:97
  8.7 8.1 %copy-start.13 = (s32[1,2]{1,0:T(1,128)S(1)}, s32[1,2]{1,0:T(1,128)}, u32[]{:S(2)}) copy-start(s32[1,2]{1,0:T(1,128)} %param.12) | copy-start | bytes 28
  8.8 16.7 %collective-permute-start.3 = (bf16[256,512]{1,0:T(8,128)(2,1)}, bf16[256,512]{1,0:T(8,128)(2,1)S(1)}, u32[]{:S(2)}, u32[]{:S(2)}) collective-permute-start(bf16[256,512]{1,0:T(8,128)(2,1)} %bitcast.19), channel_id=1, source_target_pairs={{0,4},{2,6},{4,8},{6,10},{8,12},{10,14},{12,0},{14,2},{1,13},{3,15... | collective-permute-start | bytes 786440 | tf_op jit(solution)/shard_map/ppermute | solution.py:93
  10.7 16.7 %collective-permute-start.1 = (bf16[256,512]{1,0:T(8,128)(2,1)}, bf16[256,512]{1,0:T(8,128)(2,1)S(1)}, u32[]{:S(2)}, u32[]{:S(2)}) collective-permute-start(bf16[256,512]{1,0:T(8,128)(2,1)} %bitcast.20), channel_id=1, source_target_pairs={{0,12},{2,14},{4,0},{6,2},{8,4},{10,6},{12,8},{14,10},{1,5},{3,7},... | collective-permute-start | bytes 786440 | tf_op jit(solution)/shard_map/ppermute | solution.py:93
  15.0 14.4 %collective-permute-start.6 = (bf16[256,512]{1,0:T(8,128)(2,1)}, bf16[256,512]{1,0:T(8,128)(2,1)S(1)}, u32[]{:S(2)}, u32[]{:S(2)}) collective-permute-start(bf16[256,512]{1,0:T(8,128)(2,1)} %bitcast.21), channel_id=1, source_target_pairs={{0,14},{2,0},{4,2},{6,4},{8,6},{10,8},{12,10},{14,12},{1,3},{3,5},... | collective-permute-start | bytes 786440 | tf_op jit(solution)/shard_map/ppermute | solution.py:93
  17.0 0.7 copy-start.10
  17.8 14.9 %copy-start.11 = (s32[26]{0:T(128)}, s32[26]{0:T(128)S(1)}, u32[]{:S(2)}) copy-start(s32[26]{0:T(128)S(1)} %reshape.13.own) | copy-start | bytes 316
  17.8 4.5 %collective-permute-start = (s32[26]{0:T(128)S(1)}, s32[26]{0:T(128)S(1)}, u32[]{:S(2)}, u32[]{:S(2)}) collective-permute-start(s32[26]{0:T(128)S(1)} %reshape.13.own), channel_id=1, source_target_pairs={{0,1},{1,0},{2,3},{3,2},{4,5},{5,4},{6,7},{7,6},{8,9},{9,8},{10,11... | collective-permute-start | bytes 320 | tf_op jit(solution)/shard_map/ppermute | solution.py:97
  22.3 10.4 %copy-start.12 = (s32[26]{0:T(128)}, s32[26]{0:T(128)S(1)}, u32[]{:S(2)}) copy-start(s32[26]{0:T(128)S(1)} %collective-permute-done.partner) | copy-start | bytes 316
  22.3 12.2 %collective-permute-start.7 = (bf16[256,512]{1,0:T(8,128)(2,1)}, bf16[256,512]{1,0:T(8,128)(2,1)S(1)}, u32[]{:S(2)}, u32[]{:S(2)}) collective-permute-start(bf16[256,512]{1,0:T(8,128)(2,1)} %bitcast.22), channel_id=1, source_target_pairs={{0,2},{2,4},{4,6},{6,8},{8,10},{10,12},{12,14},{14,0},{1,15},{3,1}... | collective-permute-start | bytes 786440 | tf_op jit(solution)/shard_map/ppermute | solution.py:93
  25.5 14.4 %collective-permute-start.4 = (bf16[256,512]{1,0:T(8,128)(2,1)S(1)}, bf16[256,512]{1,0:T(8,128)(2,1)S(1)}, u32[]{:S(2)}, u32[]{:S(2)}) collective-permute-start(bf16[256,512]{1,0:T(8,128)(2,1)S(1)} %collective-permute-done.3.p6), channel_id=1, source_target_pairs={{0,4},{2,6},{4,8},{6,10},{8,12},{10,14},{12,0},{14,2},{1,13},{3,15... | collective-permute-start | bytes 786440 | tf_op jit(solution)/shard_map/ppermute | solution.py:93
  27.4 12.9 %collective-permute-start.5 = (bf16[256,512]{1,0:T(8,128)(2,1)S(1)}, bf16[256,512]{1,0:T(8,128)(2,1)S(1)}, u32[]{:S(2)}, u32[]{:S(2)}) collective-permute-start(bf16[256,512]{1,0:T(8,128)(2,1)S(1)} %collective-permute-done.3.p6), channel_id=1, source_target_pairs={{0,2},{2,4},{4,6},{6,8},{8,10},{10,12},{12,14},{14,0},{1,15},{3,1}... | collective-permute-start | bytes 786440 | tf_op jit(solution)/shard_map/ppermute | solution.py:93
  29.3 13.2 %collective-permute-start.2 = (bf16[256,512]{1,0:T(8,128)(2,1)S(1)}, bf16[256,512]{1,0:T(8,128)(2,1)S(1)}, u32[]{:S(2)}, u32[]{:S(2)}) collective-permute-start(bf16[256,512]{1,0:T(8,128)(2,1)S(1)} %collective-permute-done.1.p2), channel_id=1, source_target_pairs={{0,14},{2,0},{4,2},{6,4},{8,6},{10,8},{12,10},{14,12},{1,3},{3,5},... | collective-permute-start | bytes 786440 | tf_op jit(solution)/shard_map/ppermute | solution.py:93
  34.6 1.1 copy-start
  35.7 1.0 copy-start.2
  36.7 0.9 copy-start.6
  37.7 0.7 copy-start.7
  42.5 4.9 %copy-start.1 = (bf16[1,2,12,128,128]{4,3,2,1,0:T(8,128)(2,1)S(1)}, bf16[1,2,12,128,128]{4,3,2,1,0:T(8,128)(2,1)}, u32[]{:S(2)}) copy-start(bf16[1,2,12,128,128]{4,3,2,1,0:T(8,128)(2,1)} %param.10) | copy-start | bytes 2359300
  43.4 5.6 %collective-permute-start.9 = (f32[256,512]{1,0:T(8,128)S(1)}, f32[256,512]{1,0:T(8,128)S(1)}, u32[]{:S(2)}, u32[]{:S(2)}) collective-permute-start(f32[256,512]{1,0:T(8,128)S(1)} %shard_map.93), channel_id=1, source_target_pairs={{0,1},{1,0},{2,3},{3,2},{4,5},{5,4},{6,7},{7,6},{8,9},{9,8},{10,11... | collective-permute-start | bytes 1572872 | tf_op jit(solution)/shard_map/ppermute | solution.py:97
  47.4 1.5 %copy-start.3 = (bf16[512,512]{1,0:T(8,128)(2,1)S(1)}, bf16[512,512]{1,0:T(8,128)(2,1)}, u32[]{:S(2)}) copy-start(bf16[512,512]{1,0:T(8,128)(2,1)} %w_message.2) | copy-start | bytes 1572868
  49.3 21.9 %copy-start.9 = (f32[16,512]{1,0:T(8,128)S(1)}, f32[16,512]{1,0:T(8,128)}, u32[]{:S(2)}) copy-start(f32[16,512]{1,0:T(8,128)} %taps.1) | copy-start | bytes 98308
  71.2 42.5 %copy-start.4 = (bf16[512,512]{1,0:T(8,128)(2,1)S(1)}, bf16[512,512]{1,0:T(8,128)(2,1)}, u32[]{:S(2)}) copy-start(bf16[512,512]{1,0:T(8,128)(2,1)} %w_root.3) | copy-start | bytes 1572868
  71.8 41.9 %copy-start.8 = (s32[400]{0:T(512)S(1)}, s32[400]{0:T(512)}, u32[]{:S(2)}) copy-start(s32[400]{0:T(512)} %plan.1) | copy-start | bytes 4804
  86.9 13.9 %collective-permute-start.10 = (bf16[256,512]{1,0:T(8,128)(2,1)S(1)}, bf16[256,512]{1,0:T(8,128)(2,1)S(1)}, u32[]{:S(2)}, u32[]{:S(2)}) collective-permute-start(bf16[256,512]{1,0:T(8,128)(2,1)S(1)} %bitcast.13), channel_id=1, source_target_pairs={{0,12},{2,14},{4,0},{6,2},{8,4},{10,6},{12,8},{14,10},{1,5},{3,7},... | collective-permute-start | bytes 786440 | tf_op jit(solution)/shard_map/ppermute | solution.py:93
  91.0 16.1 %collective-permute-start.12 = (bf16[256,512]{1,0:T(8,128)(2,1)S(1)}, bf16[256,512]{1,0:T(8,128)(2,1)S(1)}, u32[]{:S(2)}, u32[]{:S(2)}) collective-permute-start(bf16[256,512]{1,0:T(8,128)(2,1)S(1)} %bitcast.14), channel_id=1, source_target_pairs={{0,4},{2,6},{4,8},{6,10},{8,12},{10,14},{12,0},{14,2},{1,13},{3,15... | collective-permute-start | bytes 786440 | tf_op jit(solution)/shard_map/ppermute | solution.py:93
  94.3 19.4 %collective-permute-start.15 = (bf16[256,512]{1,0:T(8,128)(2,1)S(1)}, bf16[256,512]{1,0:T(8,128)(2,1)S(1)}, u32[]{:S(2)}, u32[]{:S(2)}) collective-permute-start(bf16[256,512]{1,0:T(8,128)(2,1)S(1)} %bitcast.15), channel_id=1, source_target_pairs={{0,14},{2,0},{4,2},{6,4},{8,6},{10,8},{12,10},{14,12},{1,3},{3,5},... | collective-permute-start | bytes 786440 | tf_op jit(solution)/shard_map/ppermute | solution.py:93
  96.7 17.0 %collective-permute-start.16 = (bf16[256,512]{1,0:T(8,128)(2,1)S(1)}, bf16[256,512]{1,0:T(8,128)(2,1)S(1)}, u32[]{:S(2)}, u32[]{:S(2)}) collective-permute-start(bf16[256,512]{1,0:T(8,128)(2,1)S(1)} %bitcast.16), channel_id=1, source_target_pairs={{0,2},{2,4},{4,6},{6,8},{8,10},{10,12},{12,14},{14,0},{1,15},{3,1}... | collective-permute-start | bytes 786440 | tf_op jit(solution)/shard_map/ppermute | solution.py:93
  100.8 14.5 %collective-permute-start.11 = (bf16[256,512]{1,0:T(8,128)(2,1)S(1)}, bf16[256,512]{1,0:T(8,128)(2,1)S(1)}, u32[]{:S(2)}, u32[]{:S(2)}) collective-permute-start(bf16[256,512]{1,0:T(8,128)(2,1)S(1)} %collective-permute-done.10.p2), channel_id=1, source_target_pairs={{0,14},{2,0},{4,2},{6,4},{8,6},{10,8},{12,10},{14,12},{1,3},{3,5},... | collective-permute-start | bytes 786440 | tf_op jit(solution)/shard_map/ppermute | solution.py:93
  107.1 13.8 %collective-permute-start.13 = (bf16[256,512]{1,0:T(8,128)(2,1)S(1)}, bf16[256,512]{1,0:T(8,128)(2,1)S(1)}, u32[]{:S(2)}, u32[]{:S(2)}) collective-permute-start(bf16[256,512]{1,0:T(8,128)(2,1)S(1)} %collective-permute-done.12.p6), channel_id=1, source_target_pairs={{0,4},{2,6},{4,8},{6,10},{8,12},{10,14},{12,0},{14,2},{1,13},{3,15... | collective-permute-start | bytes 786440 | tf_op jit(solution)/shard_map/ppermute | solution.py:93
  111.8 12.3 %collective-permute-start.14 = (bf16[256,512]{1,0:T(8,128)(2,1)S(1)}, bf16[256,512]{1,0:T(8,128)(2,1)S(1)}, u32[]{:S(2)}, u32[]{:S(2)}) collective-permute-start(bf16[256,512]{1,0:T(8,128)(2,1)S(1)} %collective-permute-done.12.p6), channel_id=1, source_target_pairs={{0,2},{2,4},{4,6},{6,8},{8,10},{10,12},{12,14},{14,0},{1,15},{3,1}... | collective-permute-start | bytes 786440 | tf_op jit(solution)/shard_map/ppermute | solution.py:93
  124.9 6.7 %collective-permute-start.17 = (f32[256,512]{1,0:T(8,128)S(1)}, f32[256,512]{1,0:T(8,128)S(1)}, u32[]{:S(2)}, u32[]{:S(2)}) collective-permute-start(f32[256,512]{1,0:T(8,128)S(1)} %shard_map.98), channel_id=1, source_target_pairs={{0,1},{1,0},{2,3},{3,2},{4,5},{5,4},{6,7},{7,6},{8,9},{9,8},{10,11... | collective-permute-start | bytes 1572872 | tf_op jit(solution)/shard_map/ppermute | solution.py:97
  130.1 1.5 %copy-start.5 = (bf16[512,512]{1,0:T(8,128)(2,1)S(1)}, bf16[512,512]{1,0:T(8,128)(2,1)}, u32[]{:S(2)}) copy-start(bf16[512,512]{1,0:T(8,128)(2,1)} %w_message.3) | copy-start | bytes 1572868

commit v2 on v1

--- a/solution.py
+++ b/solution.py
@@ -12,6 +12,7 @@
 RING = 8
 SMEM = pl.BlockSpec(memory_space=pltpu.SMEM)
 VMEM = pl.BlockSpec(memory_space=pltpu.VMEM)
+HBM = pl.BlockSpec(memory_space=pltpu.HBM)
 
 
 def call(kernel, outs, operands, specs, flops, moved, aliases={}, scratch=()):
@@ -67,12 +68,28 @@
                 )
 
 
-def early_kernel(plan, p0, p1, p2, p6, p7, own_tiles, other_tiles, w_root, mine, theirs, root):
+def early_kernel(plan, p0, p1, p2, p6, p7, own_tiles, other_tiles, w_root, *refs, fetch):
+    if fetch:
+        mine, theirs, root, tiles, w_local, sems, rows = refs
+        pairs = ((p0, rows), (own_tiles, tiles), (w_root, w_local))
+    else:
+        mine, theirs, root, w_local, sems = refs
+        rows, tiles, pairs = p0, own_tiles, ((w_root, w_local),)
+    copies = [
+        pltpu.make_async_copy(source, target, sems.at[i])
+        for i, (source, target) in enumerate(pairs)
+    ]
+    for copy in copies:
+        copy.start()
+    near = ((1, p1), (7, p7), (2, p2), (6, p6))
+    theirs[...] = jnp.zeros_like(theirs)
+    add_tiles(plan, near, {1: other_tiles}, {1: theirs})
+    for copy in copies:
+        copy.wait()
+    root[...] = jnp.dot(rows[...], w_local[...], preferred_element_type=jnp.float32)
     mine[...] = jnp.zeros_like(mine)
-    theirs[...] = jnp.zeros_like(theirs)
-    pieces = ((0, p0), (1, p1), (7, p7), (2, p2), (6, p6))
-    add_tiles(plan, pieces, {0: own_tiles, 1: other_tiles}, {0: mine, 1: theirs})
-    root[...] = jnp.dot(p0[...], w_root[...], preferred_element_type=jnp.float32)
+    add_tiles(plan, near, {0: tiles}, {0: mine})
+    add_tiles(plan, ((0, rows),), {0: tiles, 1: other_tiles}, {0: mine, 1: theirs})
 
 
 def late_kernel(plan, p3, p4, p5, tiles, sums_in, sums, *, side):
@@ -105,20 +122,34 @@
     return (own, back1, back2, back3, across, ahead3, ahead2, ahead1)
 
 
-def graph_layer(pieces, own_tiles, other_tiles, plan, w_message, w_root):
+def graph_layer(pieces, own_tiles, other_tiles, plan, w_message, w_root, fetch):
     own = pieces[0]
     rows, width = own.shape
     sums = jax.ShapeDtypeStruct((rows, width), jnp.float32)
     area = rows * width
     dense = 2 * area * width
-    mine, theirs, root = call(
-        early_kernel,
-        (sums, sums, sums),
+    outs = [sums, sums, sums]
+    scratch = [pltpu.VMEM(w_root.shape, w_root.dtype), pltpu.SemaphoreType.DMA((3,))]
+    if fetch:
+        outs.append(jax.ShapeDtypeStruct(own_tiles.shape, own_tiles.dtype))
+        scratch.append(pltpu.VMEM(own.shape, own.dtype))
+    local = HBM if fetch else VMEM
+    w_root = pltpu.with_memory_space_constraint(w_root, pltpu.HBM)
+    plan = pltpu.with_memory_space_constraint(plan, pltpu.HBM)
+    if fetch:
+        own, own_tiles = (pltpu.with_memory_space_constraint(x, pltpu.HBM) for x in (own, own_tiles))
+    results = call(
+        functools.partial(early_kernel, fetch=fetch),
+        outs,
         (plan, own, pieces[1], pieces[2], pieces[6], pieces[7], own_tiles, other_tiles, w_root),
-        [SMEM] + [VMEM] * 8,
+        [SMEM, local, VMEM, VMEM, VMEM, VMEM, local, VMEM, HBM],
         4 * dense,
         24 * area,
-    )
+        scratch=scratch,
+    )
+    mine, theirs, root = results[:3]
+    if fetch:
+        own_tiles = results[3]
     late = pieces[3:6]
 
     def finish(side, tiles, partial):
@@ -134,7 +165,7 @@
 
     received = swap(finish(1, other_tiles, theirs))
     mine = finish(0, own_tiles, mine)
-    return call(
+    out = call(
         last_kernel,
         jax.ShapeDtypeStruct((rows, width), jnp.bfloat16),
         (mine, received, root, w_message),
@@ -142,6 +173,7 @@
         dense,
         14 * area,
     )
+    return out, own_tiles
 
 
 def filter_kernel(hidden, taps, out):
@@ -194,10 +226,12 @@
         cost_estimate=pl.CostEstimate(flops=1000, bytes_accessed=4000, transcendentals=0),
         name="plan",
     )(lax.axis_index("vert").reshape(1), table, other_table)
-    hidden = graph_layer(pieces, own_tiles, other_tiles, plan, message_one, root_one)
+    hidden, own_tiles = graph_layer(
+        pieces, own_tiles, other_tiles, plan, message_one, root_one, True
+    )
     mixed = temporal(hidden, time_taps)
     pieces = ring_gather(mixed)
-    out = graph_layer(pieces, own_tiles, other_tiles, plan, message_two, root_two)
+    out, _ = graph_layer(pieces, own_tiles, other_tiles, plan, message_two, root_two, False)
     return out[None]
 
 

time: 134 us -> 133 us (level)
  local copies, waits for them, and re-layouts: 4.7 us -> 0.89 us
  Pallas kernels: 11.2 us -> 13.7 us
  waiting for transfers between devices: 16.9 us -> 19 us
  blocking collectives: 37 us -> 35.3 us
    unnamed x28 -> x14, local copies, waits for them, and re-layouts: 4.52 us -> 0.71 us
    pallas_call x9, Pallas kernels: 9.36 us -> 11.9 us  [call(): pl.pallas_call(kernel, out_shape=outs, in_specs=specs, out_specs=jax.tree...]
    ppermute x14, waiting for transfers between devices: 15.9 us -> 18.2 us  [shift(): return lax.ppermute(x, 'vert', pairs)]
  transfers between devices with their start and end apart: 18 -> 18, of which waited for: 8 -> 7; matrix products, arithmetic and copies ran while one was open for 0% -> 0% of each run, Pallas kernels for 6% -> 8%
where the time goes in v2:
time: 133 us; the launch traced here: 132 us
  starting transfers between devices  62.8 us (47%)
  blocking collectives  35.3 us (27%)
  waiting for transfers between devices  19 us (14%)
  Pallas kernels  13.7 us (10%)
    ppermute x14, starting transfers between devices, shift(): return lax.ppermute(x, 'vert', pairs)  40.2 us
    ppermute x4, starting transfers between devices, swap(): return lax.ppermute(x, 'vert', [(v, v ^ 1) for v in range(2 * RING)])  22.6 us
    all_to_all x1, blocking collectives, temporal(): by_vertex = lax.all_to_all(split, 'snap', split_axis=0, concat_axis=0)  20.6 us
    ppermute x14, waiting for transfers between devices, shift(): return lax.ppermute(x, 'vert', pairs)  18.2 us
    all_to_all x1, blocking collectives, temporal(): returned = lax.all_to_all(mixed, 'snap', split_axis=0, concat_axis=0)  14.7 us
    pallas_call x9, Pallas kernels, call(): pl.pallas_call(kernel, out_shape=outs, in_specs=specs, out_specs=jax.tree...  11.9 us
  transfers between devices with their start and end apart: 18, of which 7 were waited for; matrix products, arithmetic and copies ran while one was open for 0% of the time, Pallas kernels for 8%

profile of v2, /device:TPU:1, one launch (start us, length us, event | category | flops | bytes accessed | tf_op | source)
XLA Modules:
  0.0 132.1 jit_solution(6199698464148809882)
XLA Ops:
  0.0 8.7 %collective-permute-start.8 = (bf16[24,128,128]{2,1,0:T(8,128)(2,1)}, bf16[24,128,128]{2,1,0:T(8,128)(2,1)S(1)}, u32[]{:S(2)}, u32[]{:S(2)}) collective-permute-start(bf16[24,128,128]{2,1,0:T(8,128)(2,1)} %bitcast.14), channel_id=1, source_target_pairs={{0,1},{1,0},{2,3},{3,2},{4,5},{5,4},{6,7},{7,6},{8,9},{9,8},{10,11... | collective-permute-start | bytes 2359304 | tf_op jit(solution)/shard_map/ppermute | solution.py:114
  8.7 0.0 copy-start.6
  8.8 1.9 %collective-permute-start.3 = (bf16[256,512]{1,0:T(8,128)(2,1)}, bf16[256,512]{1,0:T(8,128)(2,1)S(1)}, u32[]{:S(2)}, u32[]{:S(2)}) collective-permute-start(bf16[256,512]{1,0:T(8,128)(2,1)} %bitcast.16), channel_id=1, source_target_pairs={{0,4},{2,6},{4,8},{6,10},{8,12},{10,14},{12,0},{14,2},{1,13},{3,15... | collective-permute-start | bytes 786440 | tf_op jit(solution)/shard_map/ppermute | solution.py:110
  10.7 4.3 %collective-permute-start.1 = (bf16[256,512]{1,0:T(8,128)(2,1)}, bf16[256,512]{1,0:T(8,128)(2,1)S(1)}, u32[]{:S(2)}, u32[]{:S(2)}) collective-permute-start(bf16[256,512]{1,0:T(8,128)(2,1)} %bitcast.17), channel_id=1, source_target_pairs={{0,12},{2,14},{4,0},{6,2},{8,4},{10,6},{12,8},{14,10},{1,5},{3,7},... | collective-permute-start | bytes 786440 | tf_op jit(solution)/shard_map/ppermute | solution.py:110
  15.0 1.9 %collective-permute-start.6 = (bf16[256,512]{1,0:T(8,128)(2,1)}, bf16[256,512]{1,0:T(8,128)(2,1)S(1)}, u32[]{:S(2)}, u32[]{:S(2)}) collective-permute-start(bf16[256,512]{1,0:T(8,128)(2,1)} %bitcast.18), channel_id=1, source_target_pairs={{0,14},{2,0},{4,2},{6,4},{8,6},{10,8},{12,10},{14,12},{1,3},{3,5},... | collective-permute-start | bytes 786440 | tf_op jit(solution)/shard_map/ppermute | solution.py:110
  16.9 0.0 copy-done.6
  16.9 0.1 copy.14
  17.0 0.0 copy-start.3
  17.0 0.7 copy-done.3
  17.7 0.1 pad_add_fusion
  17.7 0.1 reshape.13.own
  17.8 3.7 %collective-permute-start = (s32[26]{0:T(128)S(1)}, s32[26]{0:T(128)S(1)}, u32[]{:S(2)}, u32[]{:S(2)}) collective-permute-start(s32[26]{0:T(128)S(1)} %reshape.13.own), channel_id=1, source_target_pairs={{0,1},{1,0},{2,3},{3,2},{4,5},{5,4},{6,7},{7,6},{8,9},{9,8},{10,11... | collective-permute-start | bytes 320 | tf_op jit(solution)/shard_map/ppermute | solution.py:114
  21.5 0.8 collective-permute-done.partner
  22.3 0.0 copy-start.5
  22.3 3.1 %collective-permute-start.7 = (bf16[256,512]{1,0:T(8,128)(2,1)}, bf16[256,512]{1,0:T(8,128)(2,1)S(1)}, u32[]{:S(2)}, u32[]{:S(2)}) collective-permute-start(bf16[256,512]{1,0:T(8,128)(2,1)} %bitcast.19), channel_id=1, source_target_pairs={{0,2},{2,4},{4,6},{6,8},{8,10},{10,12},{12,14},{14,0},{1,15},{3,1}... | collective-permute-start | bytes 786440 | tf_op jit(solution)/shard_map/ppermute | solution.py:110
  25.4 0.0 collective-permute-done.3.p6
  25.5 1.9 %collective-permute-start.4 = (bf16[256,512]{1,0:T(8,128)(2,1)S(1)}, bf16[256,512]{1,0:T(8,128)(2,1)S(1)}, u32[]{:S(2)}, u32[]{:S(2)}) collective-permute-start(bf16[256,512]{1,0:T(8,128)(2,1)S(1)} %collective-permute-done.3.p6), channel_id=1, source_target_pairs={{0,4},{2,6},{4,8},{6,10},{8,12},{10,14},{12,0},{14,2},{1,13},{3,15... | collective-permute-start | bytes 786440 | tf_op jit(solution)/shard_map/ppermute | solution.py:110
  27.4 0.0 collective-permute-done.1.p2
  27.4 1.9 %collective-permute-start.5 = (bf16[256,512]{1,0:T(8,128)(2,1)S(1)}, bf16[256,512]{1,0:T(8,128)(2,1)S(1)}, u32[]{:S(2)}, u32[]{:S(2)}) collective-permute-start(bf16[256,512]{1,0:T(8,128)(2,1)S(1)} %collective-permute-done.3.p6), channel_id=1, source_target_pairs={{0,2},{2,4},{4,6},{6,8},{8,10},{10,12},{12,14},{14,0},{1,15},{3,1}... | collective-permute-start | bytes 786440 | tf_op jit(solution)/shard_map/ppermute | solution.py:110
  29.3 0.0 collective-permute-done.6.p1
  29.3 3.4 %collective-permute-start.2 = (bf16[256,512]{1,0:T(8,128)(2,1)S(1)}, bf16[256,512]{1,0:T(8,128)(2,1)S(1)}, u32[]{:S(2)}, u32[]{:S(2)}) collective-permute-start(bf16[256,512]{1,0:T(8,128)(2,1)S(1)} %collective-permute-done.1.p2), channel_id=1, source_target_pairs={{0,14},{2,0},{4,2},{6,4},{8,6},{10,8},{12,10},{14,12},{1,3},{3,5},... | collective-permute-start | bytes 786440 | tf_op jit(solution)/shard_map/ppermute | solution.py:110
  32.7 0.0 copy-done.4
  32.7 0.0 copy-done.5
  32.7 1.8 %plan.1 = s32[400]{0:T(512)} custom-call(s32[1]{0:T(128)} %bitcast.where, s32[26]{0:T(128)} %copy-done.4, s32[26]{0:T(128)} %copy-done.5), custom_call_target="tpu_custom_call" | custom-call | flops 1000 | bytes 4000 | tf_op jit(solution)/shard_map/plan/pallas_call | solution.py:221
  34.5 0.0 collective-permute-done.7.p7
  34.5 0.0 collective-permute-done.8.other_tiles.tiles
  34.6 2.6 %shard_map.91 = (f32[256,512]{1,0:T(8,128)S(1)}, f32[256,512]{1,0:T(8,128)S(1)}, f32[256,512]{1,0:T(8,128)S(1)}, bf16[24,128,128]{2,1,0:T(8,128)(2,1)S(1)}) custom-call(s32[400]{0:T(512)} %plan.1, bf16[256,512]{1,0:T(8,128)(2,1)} %bitcast.20, bf16[256,512]{1,0:T(8,128)(2,1)S(1)} %collective-permute-done.6.p1, ...), custom_call_target="tpu_custom_call" | custom-call | flops 536870912 | bytes 3145728 | tf_op jit(solution)/shard_map/pallas_call | solution.py:19
  37.2 0.3 collective-permute-done.4.p4
  37.5 2.8 %collective-permute-done.5.p5 = bf16[256,512]{1,0:T(8,128)(2,1)S(1)} collective-permute-done((bf16[256,512]{1,0:T(8,128)(2,1)S(1)}, bf16[256,512]{1,0:T(8,128)(2,1)S(1)}, u32[]{:S(2)}, u32[]{:S(2)}) %collective-permute-start.5) | collective-permute-done | bytes 262176 | tf_op jit(solution)/shard_map/ppermute | solution.py:110
  40.3 2.3 %collective-permute-done.2.p3 = bf16[256,512]{1,0:T(8,128)(2,1)S(1)} collective-permute-done((bf16[256,512]{1,0:T(8,128)(2,1)S(1)}, bf16[256,512]{1,0:T(8,128)(2,1)S(1)}, u32[]{:S(2)}, u32[]{:S(2)}) %collective-permute-start.2) | collective-permute-done | bytes 262176 | tf_op jit(solution)/shard_map/ppermute | solution.py:110
  42.5 1.0 shard_map.93
  43.5 4.0 %collective-permute-start.9 = (f32[256,512]{1,0:T(8,128)S(1)}, f32[256,512]{1,0:T(8,128)S(1)}, u32[]{:S(2)}, u32[]{:S(2)}) collective-permute-start(f32[256,512]{1,0:T(8,128)S(1)} %shard_map.93), channel_id=1, source_target_pairs={{0,1},{1,0},{2,3},{3,2},{4,5},{5,4},{6,7},{7,6},{8,9},{9,8},{10,11... | collective-permute-start | bytes 1572872 | tf_op jit(solution)/shard_map/ppermute | solution.py:114
  47.5 0.0 copy-start
  47.5 1.6 %shard_map.92.mine = f32[256,512]{1,0:T(8,128)S(1)} custom-call(s32[400]{0:T(512)} %plan.1, bf16[256,512]{1,0:T(8,128)(2,1)S(1)} %collective-permute-done.2.p3, bf16[256,512]{1,0:T(8,128)(2,1)S(1)} %collective-permute-done.4.p4, bf16[256,512]{1,0:T(8,128)(2,1)S(1)} %collective-permute-done.5.p5, ...), custom_call_target="tpu_custom_call", output_to_operand_aliasing={{}: (5, {})} | custom-call | flops 134217728 | bytes 1048576 | tf_op jit(solution)/shard_map/pallas_call | solution.py:19
  49.2 0.0 collective-permute-done.9.received
  49.2 0.0 copy-done
  49.2 0.3 shard_map.94
  49.5 0.0 copy-start.2
  49.5 20.6 %all_to_all.10.hidden = bf16[32,8,512]{2,1,0:T(8,128)(2,1)S(1)} all-to-all(bf16[32,8,512]{2,1,0:T(8,128)(2,1)S(1)} %bitcast.13), channel_id=1, replica_groups=mesh['snap'=32,'vert'=16] {'snap'}, dimensions={0} | all-to-all | bytes 524288 | tf_op jit(solution)/shard_map/all_to_all | solution.py:192
  70.1 0.0 copy-done.2
  70.1 0.6 shard_map.95
  70.7 14.7 %all_to_all.11 = bf16[32,8,512]{2,1,0:T(8,128)(2,1)S(1)} all-to-all(bf16[32,8,512]{2,1,0:T(8,128)(2,1)S(1)} %shard_map.95), channel_id=1, replica_groups=mesh['snap'=32,'vert'=16] {'snap'}, dimensions={0} | all-to-all | bytes 524288 | tf_op jit(solution)/shard_map/all_to_all | solution.py:201
  85.4 3.3 %collective-permute-start.10 = (bf16[256,512]{1,0:T(8,128)(2,1)S(1)}, bf16[256,512]{1,0:T(8,128)(2,1)S(1)}, u32[]{:S(2)}, u32[]{:S(2)}) collective-permute-start(bf16[256,512]{1,0:T(8,128)(2,1)S(1)} %bitcast.8), channel_id=1, source_target_pairs={{0,12},{2,14},{4,0},{6,2},{8,4},{10,6},{12,8},{14,10},{1,5},{3,7},... | collective-permute-start | bytes 786440 | tf_op jit(solution)/shard_map/ppermute | solution.py:110
  88.7 4.1 %collective-permute-start.12 = (bf16[256,512]{1,0:T(8,128)(2,1)S(1)}, bf16[256,512]{1,0:T(8,128)(2,1)S(1)}, u32[]{:S(2)}, u32[]{:S(2)}) collective-permute-start(bf16[256,512]{1,0:T(8,128)(2,1)S(1)} %bitcast.9), channel_id=1, source_target_pairs={{0,4},{2,6},{4,8},{6,10},{8,12},{10,14},{12,0},{14,2},{1,13},{3,15... | collective-permute-start | bytes 786440 | tf_op jit(solution)/shard_map/ppermute | solution.py:110
  92.8 2.2 %collective-permute-start.15 = (bf16[256,512]{1,0:T(8,128)(2,1)S(1)}, bf16[256,512]{1,0:T(8,128)(2,1)S(1)}, u32[]{:S(2)}, u32[]{:S(2)}) collective-permute-start(bf16[256,512]{1,0:T(8,128)(2,1)S(1)} %bitcast.10), channel_id=1, source_target_pairs={{0,14},{2,0},{4,2},{6,4},{8,6},{10,8},{12,10},{14,12},{1,3},{3,5},... | collective-permute-start | bytes 786440 | tf_op jit(solution)/shard_map/ppermute | solution.py:110
  94.9 4.3 %collective-permute-start.16 = (bf16[256,512]{1,0:T(8,128)(2,1)S(1)}, bf16[256,512]{1,0:T(8,128)(2,1)S(1)}, u32[]{:S(2)}, u32[]{:S(2)}) collective-permute-start(bf16[256,512]{1,0:T(8,128)(2,1)S(1)} %bitcast.11), channel_id=1, source_target_pairs={{0,2},{2,4},{4,6},{6,8},{8,10},{10,12},{12,14},{14,0},{1,15},{3,1}... | collective-permute-start | bytes 786440 | tf_op jit(solution)/shard_map/ppermute | solution.py:110
  99.3 0.0 collective-permute-done.10.p2
  99.3 1.9 %collective-permute-start.11 = (bf16[256,512]{1,0:T(8,128)(2,1)S(1)}, bf16[256,512]{1,0:T(8,128)(2,1)S(1)}, u32[]{:S(2)}, u32[]{:S(2)}) collective-permute-start(bf16[256,512]{1,0:T(8,128)(2,1)S(1)} %collective-permute-done.10.p2), channel_id=1, source_target_pairs={{0,14},{2,0},{4,2},{6,4},{8,6},{10,8},{12,10},{14,12},{1,3},{3,5},... | collective-permute-start | bytes 786440 | tf_op jit(solution)/shard_map/ppermute | solution.py:110
  101.2 4.9 %collective-permute-done.12.p6 = bf16[256,512]{1,0:T(8,128)(2,1)S(1)} collective-permute-done((bf16[256,512]{1,0:T(8,128)(2,1)S(1)}, bf16[256,512]{1,0:T(8,128)(2,1)S(1)}, u32[]{:S(2)}, u32[]{:S(2)}) %collective-permute-start.12) | collective-permute-done | bytes 262176 | tf_op jit(solution)/shard_map/ppermute | solution.py:110
  106.1 4.1 %collective-permute-start.13 = (bf16[256,512]{1,0:T(8,128)(2,1)S(1)}, bf16[256,512]{1,0:T(8,128)(2,1)S(1)}, u32[]{:S(2)}, u32[]{:S(2)}) collective-permute-start(bf16[256,512]{1,0:T(8,128)(2,1)S(1)} %collective-permute-done.12.p6), channel_id=1, source_target_pairs={{0,4},{2,6},{4,8},{6,10},{8,12},{10,14},{12,0},{14,2},{1,13},{3,15... | collective-permute-start | bytes 786440 | tf_op jit(solution)/shard_map/ppermute | solution.py:110
  110.2 1.9 %collective-permute-start.14 = (bf16[256,512]{1,0:T(8,128)(2,1)S(1)}, bf16[256,512]{1,0:T(8,128)(2,1)S(1)}, u32[]{:S(2)}, u32[]{:S(2)}) collective-permute-start(bf16[256,512]{1,0:T(8,128)(2,1)S(1)} %collective-permute-done.12.p6), channel_id=1, source_target_pairs={{0,2},{2,4},{4,6},{6,8},{8,10},{10,12},{12,14},{14,0},{1,15},{3,1}... | collective-permute-start | bytes 786440 | tf_op jit(solution)/shard_map/ppermute | solution.py:110
  112.2 0.0 collective-permute-done.15.p1
  112.2 0.0 collective-permute-done.16.p7
  112.2 2.3 %shard_map.96 = (f32[256,512]{1,0:T(8,128)S(1)}, f32[256,512]{1,0:T(8,128)S(1)}, f32[256,512]{1,0:T(8,128)S(1)}) custom-call(s32[400]{0:T(512)} %plan.1, bf16[256,512]{1,0:T(8,128)(2,1)S(1)} %bitcast.12, bf16[256,512]{1,0:T(8,128)(2,1)S(1)} %collective-permute-done.15.p1, bf16[256,512]{1,0:T(8,128)(2,1)S(1)} %collective-permute-done.10.p2, ...), custom_call_target="tpu_custom_call" | custom-call | flops 536870912 | bytes 3145728 | tf_op jit(solution)/shard_map/pallas_call | solution.py:19
  114.5 0.0 collective-permute-done.11.p3
  114.5 5.7 %collective-permute-done.13.p4 = bf16[256,512]{1,0:T(8,128)(2,1)S(1)} collective-permute-done((bf16[256,512]{1,0:T(8,128)(2,1)S(1)}, bf16[256,512]{1,0:T(8,128)(2,1)S(1)}, u32[]{:S(2)}, u32[]{:S(2)}) %collective-permute-start.13) | collective-permute-done | bytes 262176 | tf_op jit(solution)/shard_map/ppermute | solution.py:110
  120.2 2.2 %collective-permute-done.14.p5 = bf16[256,512]{1,0:T(8,128)(2,1)S(1)} collective-permute-done((bf16[256,512]{1,0:T(8,128)(2,1)S(1)}, bf16[256,512]{1,0:T(8,128)(2,1)S(1)}, u32[]{:S(2)}, u32[]{:S(2)}) %collective-permute-start.14) | collective-permute-done | bytes 262176 | tf_op jit(solution)/shard_map/ppermute | solution.py:110
  122.4 1.0 shard_map.98
  123.3 6.1 %collective-permute-start.17 = (f32[256,512]{1,0:T(8,128)S(1)}, f32[256,512]{1,0:T(8,128)S(1)}, u32[]{:S(2)}, u32[]{:S(2)}) collective-permute-start(f32[256,512]{1,0:T(8,128)S(1)} %shard_map.98), channel_id=1, source_target_pairs={{0,1},{1,0},{2,3},{3,2},{4,5},{5,4},{6,7},{7,6},{8,9},{9,8},{10,11... | collective-permute-start | bytes 1572872 | tf_op jit(solution)/shard_map/ppermute | solution.py:114
  129.5 0.0 copy-start.1
  129.5 1.6 %shard_map.97.mine = f32[256,512]{1,0:T(8,128)S(1)} custom-call(s32[400]{0:T(512)} %plan.1, bf16[256,512]{1,0:T(8,128)(2,1)S(1)} %collective-permute-done.11.p3, bf16[256,512]{1,0:T(8,128)(2,1)S(1)} %collective-permute-done.13.p4, bf16[256,512]{1,0:T(8,128)(2,1)S(1)} %collective-permute-done.14.p5, ...), custom_call_target="tpu_custom_call", output_to_operand_aliasing={{}: (5, {})} | custom-call | flops 134217728 | bytes 1048576 | tf_op jit(solution)/shard_map/pallas_call | solution.py:19
  131.1 0.0 collective-permute-done.17.received
  131.1 0.0 copy-done.1
  131.1 1.0 shard_map.99
  (1 shorter events, 0.0 us)
Async XLA Ops:
  0.0 34.5 %collective-permute-start.8 = (bf16[24,128,128]{2,1,0:T(8,128)(2,1)}, bf16[24,128,128]{2,1,0:T(8,128)(2,1)S(1)}, u32[]{:S(2)}, u32[]{:S(2)}) collective-permute-start(bf16[24,128,128]{2,1,0:T(8,128)(2,1)} %bitcast.14), channel_id=1, source_target_pairs={{0,1},{1,0},{2,3},{3,2},{4,5},{5,4},{6,7},{7,6},{8,9},{9,8},{10,11... | collective-permute-start | bytes 2359304 | tf_op jit(solution)/shard_map/ppermute | solution.py:114
  8.7 8.1 %copy-start.6 = (s32[1,2]{1,0:T(1,128)S(1)}, s32[1,2]{1,0:T(1,128)}, u32[]{:S(2)}) copy-start(s32[1,2]{1,0:T(1,128)} %param.12) | copy-start | bytes 28
  8.8 16.7 %collective-permute-start.3 = (bf16[256,512]{1,0:T(8,128)(2,1)}, bf16[256,512]{1,0:T(8,128)(2,1)S(1)}, u32[]{:S(2)}, u32[]{:S(2)}) collective-permute-start(bf16[256,512]{1,0:T(8,128)(2,1)} %bitcast.16), channel_id=1, source_target_pairs={{0,4},{2,6},{4,8},{6,10},{8,12},{10,14},{12,0},{14,2},{1,13},{3,15... | collective-permute-start | bytes 786440 | tf_op jit(solution)/shard_map/ppermute | solution.py:110
  10.7 16.7 %collective-permute-start.1 = (bf16[256,512]{1,0:T(8,128)(2,1)}, bf16[256,512]{1,0:T(8,128)(2,1)S(1)}, u32[]{:S(2)}, u32[]{:S(2)}) collective-permute-start(bf16[256,512]{1,0:T(8,128)(2,1)} %bitcast.17), channel_id=1, source_target_pairs={{0,12},{2,14},{4,0},{6,2},{8,4},{10,6},{12,8},{14,10},{1,5},{3,7},... | collective-permute-start | bytes 786440 | tf_op jit(solution)/shard_map/ppermute | solution.py:110
  15.0 14.4 %collective-permute-start.6 = (bf16[256,512]{1,0:T(8,128)(2,1)}, bf16[256,512]{1,0:T(8,128)(2,1)S(1)}, u32[]{:S(2)}, u32[]{:S(2)}) collective-permute-start(bf16[256,512]{1,0:T(8,128)(2,1)} %bitcast.18), channel_id=1, source_target_pairs={{0,14},{2,0},{4,2},{6,4},{8,6},{10,8},{12,10},{14,12},{1,3},{3,5},... | collective-permute-start | bytes 786440 | tf_op jit(solution)/shard_map/ppermute | solution.py:110
  17.0 0.7 copy-start.3
  17.8 14.9 %copy-start.4 = (s32[26]{0:T(128)}, s32[26]{0:T(128)S(1)}, u32[]{:S(2)}) copy-start(s32[26]{0:T(128)S(1)} %reshape.13.own) | copy-start | bytes 316
  17.8 4.5 %collective-permute-start = (s32[26]{0:T(128)S(1)}, s32[26]{0:T(128)S(1)}, u32[]{:S(2)}, u32[]{:S(2)}) collective-permute-start(s32[26]{0:T(128)S(1)} %reshape.13.own), channel_id=1, source_target_pairs={{0,1},{1,0},{2,3},{3,2},{4,5},{5,4},{6,7},{7,6},{8,9},{9,8},{10,11... | collective-permute-start | bytes 320 | tf_op jit(solution)/shard_map/ppermute | solution.py:114
  22.3 10.4 %copy-start.5 = (s32[26]{0:T(128)}, s32[26]{0:T(128)S(1)}, u32[]{:S(2)}) copy-start(s32[26]{0:T(128)S(1)} %collective-permute-done.partner) | copy-start | bytes 316
  22.3 12.2 %collective-permute-start.7 = (bf16[256,512]{1,0:T(8,128)(2,1)}, bf16[256,512]{1,0:T(8,128)(2,1)S(1)}, u32[]{:S(2)}, u32[]{:S(2)}) collective-permute-start(bf16[256,512]{1,0:T(8,128)(2,1)} %bitcast.19), channel_id=1, source_target_pairs={{0,2},{2,4},{4,6},{6,8},{8,10},{10,12},{12,14},{14,0},{1,15},{3,1}... | collective-permute-start | bytes 786440 | tf_op jit(solution)/shard_map/ppermute | solution.py:110
  25.5 12.0 %collective-permute-start.4 = (bf16[256,512]{1,0:T(8,128)(2,1)S(1)}, bf16[256,512]{1,0:T(8,128)(2,1)S(1)}, u32[]{:S(2)}, u32[]{:S(2)}) collective-permute-start(bf16[256,512]{1,0:T(8,128)(2,1)S(1)} %collective-permute-done.3.p6), channel_id=1, source_target_pairs={{0,4},{2,6},{4,8},{6,10},{8,12},{10,14},{12,0},{14,2},{1,13},{3,15... | collective-permute-start | bytes 786440 | tf_op jit(solution)/shard_map/ppermute | solution.py:110
  27.4 12.9 %collective-permute-start.5 = (bf16[256,512]{1,0:T(8,128)(2,1)S(1)}, bf16[256,512]{1,0:T(8,128)(2,1)S(1)}, u32[]{:S(2)}, u32[]{:S(2)}) collective-permute-start(bf16[256,512]{1,0:T(8,128)(2,1)S(1)} %collective-permute-done.3.p6), channel_id=1, source_target_pairs={{0,2},{2,4},{4,6},{6,8},{8,10},{10,12},{12,14},{14,0},{1,15},{3,1}... | collective-permute-start | bytes 786440 | tf_op jit(solution)/shard_map/ppermute | solution.py:110
  29.3 13.2 %collective-permute-start.2 = (bf16[256,512]{1,0:T(8,128)(2,1)S(1)}, bf16[256,512]{1,0:T(8,128)(2,1)S(1)}, u32[]{:S(2)}, u32[]{:S(2)}) collective-permute-start(bf16[256,512]{1,0:T(8,128)(2,1)S(1)} %collective-permute-done.1.p2), channel_id=1, source_target_pairs={{0,14},{2,0},{4,2},{6,4},{8,6},{10,8},{12,10},{14,12},{1,3},{3,5},... | collective-permute-start | bytes 786440 | tf_op jit(solution)/shard_map/ppermute | solution.py:110
  43.5 5.7 %collective-permute-start.9 = (f32[256,512]{1,0:T(8,128)S(1)}, f32[256,512]{1,0:T(8,128)S(1)}, u32[]{:S(2)}, u32[]{:S(2)}) collective-permute-start(f32[256,512]{1,0:T(8,128)S(1)} %shard_map.93), channel_id=1, source_target_pairs={{0,1},{1,0},{2,3},{3,2},{4,5},{5,4},{6,7},{7,6},{8,9},{9,8},{10,11... | collective-permute-start | bytes 1572872 | tf_op jit(solution)/shard_map/ppermute | solution.py:114
  47.5 1.6 %copy-start = (bf16[512,512]{1,0:T(8,128)(2,1)S(1)}, bf16[512,512]{1,0:T(8,128)(2,1)}, u32[]{:S(2)}) copy-start(bf16[512,512]{1,0:T(8,128)(2,1)} %w_message.2) | copy-start | bytes 1572868
  49.5 20.6 %copy-start.2 = (f32[16,512]{1,0:T(8,128)S(1)}, f32[16,512]{1,0:T(8,128)}, u32[]{:S(2)}) copy-start(f32[16,512]{1,0:T(8,128)} %taps.1) | copy-start | bytes 98308
  85.4 13.9 %collective-permute-start.10 = (bf16[256,512]{1,0:T(8,128)(2,1)S(1)}, bf16[256,512]{1,0:T(8,128)(2,1)S(1)}, u32[]{:S(2)}, u32[]{:S(2)}) collective-permute-start(bf16[256,512]{1,0:T(8,128)(2,1)S(1)} %bitcast.8), channel_id=1, source_target_pairs={{0,12},{2,14},{4,0},{6,2},{8,4},{10,6},{12,8},{14,10},{1,5},{3,7},... | collective-permute-start | bytes 786440 | tf_op jit(solution)/shard_map/ppermute | solution.py:110
  88.7 17.4 %collective-permute-start.12 = (bf16[256,512]{1,0:T(8,128)(2,1)S(1)}, bf16[256,512]{1,0:T(8,128)(2,1)S(1)}, u32[]{:S(2)}, u32[]{:S(2)}) collective-permute-start(bf16[256,512]{1,0:T(8,128)(2,1)S(1)} %bitcast.9), channel_id=1, source_target_pairs={{0,4},{2,6},{4,8},{6,10},{8,12},{10,14},{12,0},{14,2},{1,13},{3,15... | collective-permute-start | bytes 786440 | tf_op jit(solution)/shard_map/ppermute | solution.py:110
  92.8 19.4 %collective-permute-start.15 = (bf16[256,512]{1,0:T(8,128)(2,1)S(1)}, bf16[256,512]{1,0:T(8,128)(2,1)S(1)}, u32[]{:S(2)}, u32[]{:S(2)}) collective-permute-start(bf16[256,512]{1,0:T(8,128)(2,1)S(1)} %bitcast.10), channel_id=1, source_target_pairs={{0,14},{2,0},{4,2},{6,4},{8,6},{10,8},{12,10},{14,12},{1,3},{3,5},... | collective-permute-start | bytes 786440 | tf_op jit(solution)/shard_map/ppermute | solution.py:110
  94.9 17.2 %collective-permute-start.16 = (bf16[256,512]{1,0:T(8,128)(2,1)S(1)}, bf16[256,512]{1,0:T(8,128)(2,1)S(1)}, u32[]{:S(2)}, u32[]{:S(2)}) collective-permute-start(bf16[256,512]{1,0:T(8,128)(2,1)S(1)} %bitcast.11), channel_id=1, source_target_pairs={{0,2},{2,4},{4,6},{6,8},{8,10},{10,12},{12,14},{14,0},{1,15},{3,1}... | collective-permute-start | bytes 786440 | tf_op jit(solution)/shard_map/ppermute | solution.py:110
  99.3 15.2 %collective-permute-start.11 = (bf16[256,512]{1,0:T(8,128)(2,1)S(1)}, bf16[256,512]{1,0:T(8,128)(2,1)S(1)}, u32[]{:S(2)}, u32[]{:S(2)}) collective-permute-start(bf16[256,512]{1,0:T(8,128)(2,1)S(1)} %collective-permute-done.10.p2), channel_id=1, source_target_pairs={{0,14},{2,0},{4,2},{6,4},{8,6},{10,8},{12,10},{14,12},{1,3},{3,5},... | collective-permute-start | bytes 786440 | tf_op jit(solution)/shard_map/ppermute | solution.py:110
  106.1 14.0 %collective-permute-start.13 = (bf16[256,512]{1,0:T(8,128)(2,1)S(1)}, bf16[256,512]{1,0:T(8,128)(2,1)S(1)}, u32[]{:S(2)}, u32[]{:S(2)}) collective-permute-start(bf16[256,512]{1,0:T(8,128)(2,1)S(1)} %collective-permute-done.12.p6), channel_id=1, source_target_pairs={{0,4},{2,6},{4,8},{6,10},{8,12},{10,14},{12,0},{14,2},{1,13},{3,15... | collective-permute-start | bytes 786440 | tf_op jit(solution)/shard_map/ppermute | solution.py:110
  110.2 12.2 %collective-permute-start.14 = (bf16[256,512]{1,0:T(8,128)(2,1)S(1)}, bf16[256,512]{1,0:T(8,128)(2,1)S(1)}, u32[]{:S(2)}, u32[]{:S(2)}) collective-permute-start(bf16[256,512]{1,0:T(8,128)(2,1)S(1)} %collective-permute-done.12.p6), channel_id=1, source_target_pairs={{0,2},{2,4},{4,6},{6,8},{8,10},{10,12},{12,14},{14,0},{1,15},{3,1}... | collective-permute-start | bytes 786440 | tf_op jit(solution)/shard_map/ppermute | solution.py:110
  123.3 7.8 %collective-permute-start.17 = (f32[256,512]{1,0:T(8,128)S(1)}, f32[256,512]{1,0:T(8,128)S(1)}, u32[]{:S(2)}, u32[]{:S(2)}) collective-permute-start(f32[256,512]{1,0:T(8,128)S(1)} %shard_map.98), channel_id=1, source_target_pairs={{0,1},{1,0},{2,3},{3,2},{4,5},{5,4},{6,7},{7,6},{8,9},{9,8},{10,11... | collective-permute-start | bytes 1572872 | tf_op jit(solution)/shard_map/ppermute | solution.py:114
  129.5 1.6 %copy-start.1 = (bf16[512,512]{1,0:T(8,128)(2,1)S(1)}, bf16[512,512]{1,0:T(8,128)(2,1)}, u32[]{:S(2)}) copy-start(bf16[512,512]{1,0:T(8,128)(2,1)} %w_message.3) | copy-start | bytes 1572868

commit v3 on v2

--- a/solution.py
+++ b/solution.py
@@ -29,7 +29,7 @@
 
 
 def plan_kernel(slots, where, own, partner, plan):
-    y, core = where[0] // 2, where[0] % 2
+    y, core = where[0] >> 1, where[0] & 1
     lists = 2 * RING
     for i in range(lists):
         plan[i] = 0
@@ -39,16 +39,16 @@
             @pl.loop(0, table[r * (slots + 1) + slots])
             def _(k):
                 column = table[r * (slots + 1) + k]
-                step = (column // 4 - y) * (1 - 2 * core)
-                near = lax.rem(step + RING, RING) * 2 + side
-
-                @pl.when(lax.rem(column // 2, 2) == core)
+                near = (((column >> 2) - y) * (1 - 2 * core)) & (RING - 1)
+                index = near * 2 + side
+
+                @pl.when(((column >> 1) & 1) == core)
                 def _():
-                    filled = plan[near]
-                    plan[lists + near * 2 * slots + filled] = (r * slots + k) * 2 + lax.rem(
-                        column, 2
+                    filled = plan[index]
+                    plan[lists + index * 2 * slots + filled] = (
+                        ((r * slots + k) << 2) + r * 2 + (column & 1)
                     )
-                    plan[near] = filled + 1
+                    plan[index] = filled + 1
 
 
 def add_tiles(plan, pieces, tiles, sums):
@@ -60,11 +60,10 @@
             @pl.loop(0, plan[index])
             def _(i):
                 entry = plan[2 * RING + index * 2 * slots + i]
-                half, slot = lax.rem(entry, 2), entry // 2
-                rows = pl.ds(pl.multiple_of(slot // slots * TILE, TILE), TILE)
-                block = pl.ds(pl.multiple_of(half * TILE, TILE), TILE)
+                rows = pl.ds(pl.multiple_of(((entry >> 1) & 1) * TILE, TILE), TILE)
+                block = pl.ds(pl.multiple_of((entry & 1) * TILE, TILE), TILE)
                 sums[side][rows, :] += jnp.dot(
-                    tiles[side][slot], piece[block, :], preferred_element_type=jnp.float32
+                    tiles[side][entry >> 2], piece[block, :], preferred_element_type=jnp.float32
                 )
 
 

time: 133 us -> 133 us (level)
  transfers between devices with their start and end apart: 18 -> 18, of which waited for: 7 -> 7; matrix products, arithmetic and copies ran while one was open for 0% -> 0% of each run, Pallas kernels for 8% -> 7%
where the time goes in v3:
time: 133 us; the launch traced here: 132 us
  starting transfers between devices  62.8 us (47%)
  blocking collectives  35.3 us (27%)
  waiting for transfers between devices  19.2 us (14%)
  Pallas kernels  13.5 us (10%)
    ppermute x14, starting transfers between devices, shift(): return lax.ppermute(x, 'vert', pairs)  40.2 us
    ppermute x4, starting transfers between devices, swap(): return lax.ppermute(x, 'vert', [(v, v ^ 1) for v in range(2 * RING)])  22.6 us
    all_to_all x1, blocking collectives, temporal(): by_vertex = lax.all_to_all(split, 'snap', split_axis=0, concat_axis=0)  20.6 us
    ppermute x14, waiting for transfers between devices, shift(): return lax.ppermute(x, 'vert', pairs)  18.4 us
    all_to_all x1, blocking collectives, temporal(): returned = lax.all_to_all(mixed, 'snap', split_axis=0, concat_axis=0)  14.7 us
    pallas_call x9, Pallas kernels, call(): pl.pallas_call(kernel, out_shape=outs, in_specs=specs, out_specs=jax.tree...  11.9 us
  transfers between devices with their start and end apart: 18, of which 7 were waited for; matrix products, arithmetic and copies ran while one was open for 0% of the time, Pallas kernels for 7%

profile of v3, /device:TPU:1, one launch (start us, length us, event | category | flops | bytes accessed | tf_op | source)
XLA Modules:
  0.0 132.1 jit_solution(12589038365351486143)
XLA Ops:
  0.0 8.7 %collective-permute-start.8 = (bf16[24,128,128]{2,1,0:T(8,128)(2,1)}, bf16[24,128,128]{2,1,0:T(8,128)(2,1)S(1)}, u32[]{:S(2)}, u32[]{:S(2)}) collective-permute-start(bf16[24,128,128]{2,1,0:T(8,128)(2,1)} %bitcast.14), channel_id=1, source_target_pairs={{0,1},{1,0},{2,3},{3,2},{4,5},{5,4},{6,7},{7,6},{8,9},{9,8},{10,11... | collective-permute-start | bytes 2359304 | tf_op jit(solution)/shard_map/ppermute | solution.py:113
  8.7 0.0 copy-start.6
  8.8 1.9 %collective-permute-start.3 = (bf16[256,512]{1,0:T(8,128)(2,1)}, bf16[256,512]{1,0:T(8,128)(2,1)S(1)}, u32[]{:S(2)}, u32[]{:S(2)}) collective-permute-start(bf16[256,512]{1,0:T(8,128)(2,1)} %bitcast.16), channel_id=1, source_target_pairs={{0,4},{2,6},{4,8},{6,10},{8,12},{10,14},{12,0},{14,2},{1,13},{3,15... | collective-permute-start | bytes 786440 | tf_op jit(solution)/shard_map/ppermute | solution.py:109
  10.7 4.3 %collective-permute-start.1 = (bf16[256,512]{1,0:T(8,128)(2,1)}, bf16[256,512]{1,0:T(8,128)(2,1)S(1)}, u32[]{:S(2)}, u32[]{:S(2)}) collective-permute-start(bf16[256,512]{1,0:T(8,128)(2,1)} %bitcast.17), channel_id=1, source_target_pairs={{0,12},{2,14},{4,0},{6,2},{8,4},{10,6},{12,8},{14,10},{1,5},{3,7},... | collective-permute-start | bytes 786440 | tf_op jit(solution)/shard_map/ppermute | solution.py:109
  15.0 1.9 %collective-permute-start.6 = (bf16[256,512]{1,0:T(8,128)(2,1)}, bf16[256,512]{1,0:T(8,128)(2,1)S(1)}, u32[]{:S(2)}, u32[]{:S(2)}) collective-permute-start(bf16[256,512]{1,0:T(8,128)(2,1)} %bitcast.18), channel_id=1, source_target_pairs={{0,14},{2,0},{4,2},{6,4},{8,6},{10,8},{12,10},{14,12},{1,3},{3,5},... | collective-permute-start | bytes 786440 | tf_op jit(solution)/shard_map/ppermute | solution.py:109
  16.9 0.0 copy-done.6
  16.9 0.1 copy.14
  17.0 0.0 copy-start.3
  17.0 0.7 copy-done.3
  17.7 0.1 pad_add_fusion
  17.7 0.1 reshape.13.own
  17.8 3.7 %collective-permute-start = (s32[26]{0:T(128)S(1)}, s32[26]{0:T(128)S(1)}, u32[]{:S(2)}, u32[]{:S(2)}) collective-permute-start(s32[26]{0:T(128)S(1)} %reshape.13.own), channel_id=1, source_target_pairs={{0,1},{1,0},{2,3},{3,2},{4,5},{5,4},{6,7},{7,6},{8,9},{9,8},{10,11... | collective-permute-start | bytes 320 | tf_op jit(solution)/shard_map/ppermute | solution.py:113
  21.5 0.8 collective-permute-done.partner
  22.3 0.0 copy-start.5
  22.3 3.1 %collective-permute-start.7 = (bf16[256,512]{1,0:T(8,128)(2,1)}, bf16[256,512]{1,0:T(8,128)(2,1)S(1)}, u32[]{:S(2)}, u32[]{:S(2)}) collective-permute-start(bf16[256,512]{1,0:T(8,128)(2,1)} %bitcast.19), channel_id=1, source_target_pairs={{0,2},{2,4},{4,6},{6,8},{8,10},{10,12},{12,14},{14,0},{1,15},{3,1}... | collective-permute-start | bytes 786440 | tf_op jit(solution)/shard_map/ppermute | solution.py:109
  25.4 0.0 collective-permute-done.3.p6
  25.5 1.9 %collective-permute-start.4 = (bf16[256,512]{1,0:T(8,128)(2,1)S(1)}, bf16[256,512]{1,0:T(8,128)(2,1)S(1)}, u32[]{:S(2)}, u32[]{:S(2)}) collective-permute-start(bf16[256,512]{1,0:T(8,128)(2,1)S(1)} %collective-permute-done.3.p6), channel_id=1, source_target_pairs={{0,4},{2,6},{4,8},{6,10},{8,12},{10,14},{12,0},{14,2},{1,13},{3,15... | collective-permute-start | bytes 786440 | tf_op jit(solution)/shard_map/ppermute | solution.py:109
  27.4 0.0 collective-permute-done.1.p2
  27.4 1.9 %collective-permute-start.5 = (bf16[256,512]{1,0:T(8,128)(2,1)S(1)}, bf16[256,512]{1,0:T(8,128)(2,1)S(1)}, u32[]{:S(2)}, u32[]{:S(2)}) collective-permute-start(bf16[256,512]{1,0:T(8,128)(2,1)S(1)} %collective-permute-done.3.p6), channel_id=1, source_target_pairs={{0,2},{2,4},{4,6},{6,8},{8,10},{10,12},{12,14},{14,0},{1,15},{3,1}... | collective-permute-start | bytes 786440 | tf_op jit(solution)/shard_map/ppermute | solution.py:109
  29.3 0.0 collective-permute-done.6.p1
  29.3 3.4 %collective-permute-start.2 = (bf16[256,512]{1,0:T(8,128)(2,1)S(1)}, bf16[256,512]{1,0:T(8,128)(2,1)S(1)}, u32[]{:S(2)}, u32[]{:S(2)}) collective-permute-start(bf16[256,512]{1,0:T(8,128)(2,1)S(1)} %collective-permute-done.1.p2), channel_id=1, source_target_pairs={{0,14},{2,0},{4,2},{6,4},{8,6},{10,8},{12,10},{14,12},{1,3},{3,5},... | collective-permute-start | bytes 786440 | tf_op jit(solution)/shard_map/ppermute | solution.py:109
  32.7 0.0 copy-done.4
  32.7 0.0 copy-done.5
  32.7 1.6 %plan.1 = s32[400]{0:T(512)} custom-call(s32[1]{0:T(128)} %bitcast.where, s32[26]{0:T(128)} %copy-done.4, s32[26]{0:T(128)} %copy-done.5), custom_call_target="tpu_custom_call" | custom-call | flops 1000 | bytes 4000 | tf_op jit(solution)/shard_map/plan/pallas_call | solution.py:220
  34.3 0.0 collective-permute-done.7.p7
  34.3 0.0 collective-permute-done.8.other_tiles.tiles
  34.3 2.6 %shard_map.91 = (f32[256,512]{1,0:T(8,128)S(1)}, f32[256,512]{1,0:T(8,128)S(1)}, f32[256,512]{1,0:T(8,128)S(1)}, bf16[24,128,128]{2,1,0:T(8,128)(2,1)S(1)}) custom-call(s32[400]{0:T(512)} %plan.1, bf16[256,512]{1,0:T(8,128)(2,1)} %bitcast.20, bf16[256,512]{1,0:T(8,128)(2,1)S(1)} %collective-permute-done.6.p1, ...), custom_call_target="tpu_custom_call" | custom-call | flops 536870912 | bytes 3145728 | tf_op jit(solution)/shard_map/pallas_call | solution.py:19
  37.0 0.5 collective-permute-done.4.p4
  37.5 2.8 %collective-permute-done.5.p5 = bf16[256,512]{1,0:T(8,128)(2,1)S(1)} collective-permute-done((bf16[256,512]{1,0:T(8,128)(2,1)S(1)}, bf16[256,512]{1,0:T(8,128)(2,1)S(1)}, u32[]{:S(2)}, u32[]{:S(2)}) %collective-permute-start.5) | collective-permute-done | bytes 262176 | tf_op jit(solution)/shard_map/ppermute | solution.py:109
  40.3 2.3 %collective-permute-done.2.p3 = bf16[256,512]{1,0:T(8,128)(2,1)S(1)} collective-permute-done((bf16[256,512]{1,0:T(8,128)(2,1)S(1)}, bf16[256,512]{1,0:T(8,128)(2,1)S(1)}, u32[]{:S(2)}, u32[]{:S(2)}) %collective-permute-start.2) | collective-permute-done | bytes 262176 | tf_op jit(solution)/shard_map/ppermute | solution.py:109
  42.5 0.9 shard_map.93
  43.5 4.0 %collective-permute-start.9 = (f32[256,512]{1,0:T(8,128)S(1)}, f32[256,512]{1,0:T(8,128)S(1)}, u32[]{:S(2)}, u32[]{:S(2)}) collective-permute-start(f32[256,512]{1,0:T(8,128)S(1)} %shard_map.93), channel_id=1, source_target_pairs={{0,1},{1,0},{2,3},{3,2},{4,5},{5,4},{6,7},{7,6},{8,9},{9,8},{10,11... | collective-permute-start | bytes 1572872 | tf_op jit(solution)/shard_map/ppermute | solution.py:113
  47.5 0.0 copy-start
  47.5 1.6 %shard_map.92.mine = f32[256,512]{1,0:T(8,128)S(1)} custom-call(s32[400]{0:T(512)} %plan.1, bf16[256,512]{1,0:T(8,128)(2,1)S(1)} %collective-permute-done.2.p3, bf16[256,512]{1,0:T(8,128)(2,1)S(1)} %collective-permute-done.4.p4, bf16[256,512]{1,0:T(8,128)(2,1)S(1)} %collective-permute-done.5.p5, ...), custom_call_target="tpu_custom_call", output_to_operand_aliasing={{}: (5, {})} | custom-call | flops 134217728 | bytes 1048576 | tf_op jit(solution)/shard_map/pallas_call | solution.py:19
  49.1 0.0 collective-permute-done.9.received
  49.2 0.0 copy-done
  49.2 0.3 shard_map.94
  49.5 0.0 copy-start.2
  49.5 20.6 %all_to_all.10.hidden = bf16[32,8,512]{2,1,0:T(8,128)(2,1)S(1)} all-to-all(bf16[32,8,512]{2,1,0:T(8,128)(2,1)S(1)} %bitcast.13), channel_id=1, replica_groups=mesh['snap'=32,'vert'=16] {'snap'}, dimensions={0} | all-to-all | bytes 524288 | tf_op jit(solution)/shard_map/all_to_all | solution.py:191
  70.0 0.0 copy-done.2
  70.1 0.6 shard_map.95
  70.6 14.7 %all_to_all.11 = bf16[32,8,512]{2,1,0:T(8,128)(2,1)S(1)} all-to-all(bf16[32,8,512]{2,1,0:T(8,128)(2,1)S(1)} %shard_map.95), channel_id=1, replica_groups=mesh['snap'=32,'vert'=16] {'snap'}, dimensions={0} | all-to-all | bytes 524288 | tf_op jit(solution)/shard_map/all_to_all | solution.py:200
  85.4 3.3 %collective-permute-start.10 = (bf16[256,512]{1,0:T(8,128)(2,1)S(1)}, bf16[256,512]{1,0:T(8,128)(2,1)S(1)}, u32[]{:S(2)}, u32[]{:S(2)}) collective-permute-start(bf16[256,512]{1,0:T(8,128)(2,1)S(1)} %bitcast.8), channel_id=1, source_target_pairs={{0,12},{2,14},{4,0},{6,2},{8,4},{10,6},{12,8},{14,10},{1,5},{3,7},... | collective-permute-start | bytes 786440 | tf_op jit(solution)/shard_map/ppermute | solution.py:109
  88.7 4.1 %collective-permute-start.12 = (bf16[256,512]{1,0:T(8,128)(2,1)S(1)}, bf16[256,512]{1,0:T(8,128)(2,1)S(1)}, u32[]{:S(2)}, u32[]{:S(2)}) collective-permute-start(bf16[256,512]{1,0:T(8,128)(2,1)S(1)} %bitcast.9), channel_id=1, source_target_pairs={{0,4},{2,6},{4,8},{6,10},{8,12},{10,14},{12,0},{14,2},{1,13},{3,15... | collective-permute-start | bytes 786440 | tf_op jit(solution)/shard_map/ppermute | solution.py:109
  92.8 2.2 %collective-permute-start.15 = (bf16[256,512]{1,0:T(8,128)(2,1)S(1)}, bf16[256,512]{1,0:T(8,128)(2,1)S(1)}, u32[]{:S(2)}, u32[]{:S(2)}) collective-permute-start(bf16[256,512]{1,0:T(8,128)(2,1)S(1)} %bitcast.10), channel_id=1, source_target_pairs={{0,14},{2,0},{4,2},{6,4},{8,6},{10,8},{12,10},{14,12},{1,3},{3,5},... | collective-permute-start | bytes 786440 | tf_op jit(solution)/shard_map/ppermute | solution.py:109
  94.9 4.3 %collective-permute-start.16 = (bf16[256,512]{1,0:T(8,128)(2,1)S(1)}, bf16[256,512]{1,0:T(8,128)(2,1)S(1)}, u32[]{:S(2)}, u32[]{:S(2)}) collective-permute-start(bf16[256,512]{1,0:T(8,128)(2,1)S(1)} %bitcast.11), channel_id=1, source_target_pairs={{0,2},{2,4},{4,6},{6,8},{8,10},{10,12},{12,14},{14,0},{1,15},{3,1}... | collective-permute-start | bytes 786440 | tf_op jit(solution)/shard_map/ppermute | solution.py:109
  99.3 0.0 collective-permute-done.10.p2
  99.3 1.9 %collective-permute-start.11 = (bf16[256,512]{1,0:T(8,128)(2,1)S(1)}, bf16[256,512]{1,0:T(8,128)(2,1)S(1)}, u32[]{:S(2)}, u32[]{:S(2)}) collective-permute-start(bf16[256,512]{1,0:T(8,128)(2,1)S(1)} %collective-permute-done.10.p2), channel_id=1, source_target_pairs={{0,14},{2,0},{4,2},{6,4},{8,6},{10,8},{12,10},{14,12},{1,3},{3,5},... | collective-permute-start | bytes 786440 | tf_op jit(solution)/shard_map/ppermute | solution.py:109
  101.2 4.9 %collective-permute-done.12.p6 = bf16[256,512]{1,0:T(8,128)(2,1)S(1)} collective-permute-done((bf16[256,512]{1,0:T(8,128)(2,1)S(1)}, bf16[256,512]{1,0:T(8,128)(2,1)S(1)}, u32[]{:S(2)}, u32[]{:S(2)}) %collective-permute-start.12) | collective-permute-done | bytes 262176 | tf_op jit(solution)/shard_map/ppermute | solution.py:109
  106.1 4.1 %collective-permute-start.13 = (bf16[256,512]{1,0:T(8,128)(2,1)S(1)}, bf16[256,512]{1,0:T(8,128)(2,1)S(1)}, u32[]{:S(2)}, u32[]{:S(2)}) collective-permute-start(bf16[256,512]{1,0:T(8,128)(2,1)S(1)} %collective-permute-done.12.p6), channel_id=1, source_target_pairs={{0,4},{2,6},{4,8},{6,10},{8,12},{10,14},{12,0},{14,2},{1,13},{3,15... | collective-permute-start | bytes 786440 | tf_op jit(solution)/shard_map/ppermute | solution.py:109
  110.2 1.9 %collective-permute-start.14 = (bf16[256,512]{1,0:T(8,128)(2,1)S(1)}, bf16[256,512]{1,0:T(8,128)(2,1)S(1)}, u32[]{:S(2)}, u32[]{:S(2)}) collective-permute-start(bf16[256,512]{1,0:T(8,128)(2,1)S(1)} %collective-permute-done.12.p6), channel_id=1, source_target_pairs={{0,2},{2,4},{4,6},{6,8},{8,10},{10,12},{12,14},{14,0},{1,15},{3,1}... | collective-permute-start | bytes 786440 | tf_op jit(solution)/shard_map/ppermute | solution.py:109
  112.1 0.0 collective-permute-done.15.p1
  112.1 0.0 collective-permute-done.16.p7
  112.2 2.3 %shard_map.96 = (f32[256,512]{1,0:T(8,128)S(1)}, f32[256,512]{1,0:T(8,128)S(1)}, f32[256,512]{1,0:T(8,128)S(1)}) custom-call(s32[400]{0:T(512)} %plan.1, bf16[256,512]{1,0:T(8,128)(2,1)S(1)} %bitcast.12, bf16[256,512]{1,0:T(8,128)(2,1)S(1)} %collective-permute-done.15.p1, bf16[256,512]{1,0:T(8,128)(2,1)S(1)} %collective-permute-done.10.p2, ...), custom_call_target="tpu_custom_call" | custom-call | flops 536870912 | bytes 3145728 | tf_op jit(solution)/shard_map/pallas_call | solution.py:19
  114.4 0.0 collective-permute-done.11.p3
  114.5 5.7 %collective-permute-done.13.p4 = bf16[256,512]{1,0:T(8,128)(2,1)S(1)} collective-permute-done((bf16[256,512]{1,0:T(8,128)(2,1)S(1)}, bf16[256,512]{1,0:T(8,128)(2,1)S(1)}, u32[]{:S(2)}, u32[]{:S(2)}) %collective-permute-start.13) | collective-permute-done | bytes 262176 | tf_op jit(solution)/shard_map/ppermute | solution.py:109
  120.2 2.2 %collective-permute-done.14.p5 = bf16[256,512]{1,0:T(8,128)(2,1)S(1)} collective-permute-done((bf16[256,512]{1,0:T(8,128)(2,1)S(1)}, bf16[256,512]{1,0:T(8,128)(2,1)S(1)}, u32[]{:S(2)}, u32[]{:S(2)}) %collective-permute-start.14) | collective-permute-done | bytes 262176 | tf_op jit(solution)/shard_map/ppermute | solution.py:109
  122.4 1.0 shard_map.98
  123.3 6.1 %collective-permute-start.17 = (f32[256,512]{1,0:T(8,128)S(1)}, f32[256,512]{1,0:T(8,128)S(1)}, u32[]{:S(2)}, u32[]{:S(2)}) collective-permute-start(f32[256,512]{1,0:T(8,128)S(1)} %shard_map.98), channel_id=1, source_target_pairs={{0,1},{1,0},{2,3},{3,2},{4,5},{5,4},{6,7},{7,6},{8,9},{9,8},{10,11... | collective-permute-start | bytes 1572872 | tf_op jit(solution)/shard_map/ppermute | solution.py:113
  129.5 0.0 copy-start.1
  129.5 1.6 %shard_map.97.mine = f32[256,512]{1,0:T(8,128)S(1)} custom-call(s32[400]{0:T(512)} %plan.1, bf16[256,512]{1,0:T(8,128)(2,1)S(1)} %collective-permute-done.11.p3, bf16[256,512]{1,0:T(8,128)(2,1)S(1)} %collective-permute-done.13.p4, bf16[256,512]{1,0:T(8,128)(2,1)S(1)} %collective-permute-done.14.p5, ...), custom_call_target="tpu_custom_call", output_to_operand_aliasing={{}: (5, {})} | custom-call | flops 134217728 | bytes 1048576 | tf_op jit(solution)/shard_map/pallas_call | solution.py:19
  131.1 0.0 collective-permute-done.17.received
  131.1 0.0 copy-done.1
  131.1 1.0 shard_map.99
  (1 shorter events, 0.0 us)
Async XLA Ops:
  0.0 34.3 %collective-permute-start.8 = (bf16[24,128,128]{2,1,0:T(8,128)(2,1)}, bf16[24,128,128]{2,1,0:T(8,128)(2,1)S(1)}, u32[]{:S(2)}, u32[]{:S(2)}) collective-permute-start(bf16[24,128,128]{2,1,0:T(8,128)(2,1)} %bitcast.14), channel_id=1, source_target_pairs={{0,1},{1,0},{2,3},{3,2},{4,5},{5,4},{6,7},{7,6},{8,9},{9,8},{10,11... | collective-permute-start | bytes 2359304 | tf_op jit(solution)/shard_map/ppermute | solution.py:113
  8.7 8.1 %copy-start.6 = (s32[1,2]{1,0:T(1,128)S(1)}, s32[1,2]{1,0:T(1,128)}, u32[]{:S(2)}) copy-start(s32[1,2]{1,0:T(1,128)} %param.12) | copy-start | bytes 28
  8.8 16.7 %collective-permute-start.3 = (bf16[256,512]{1,0:T(8,128)(2,1)}, bf16[256,512]{1,0:T(8,128)(2,1)S(1)}, u32[]{:S(2)}, u32[]{:S(2)}) collective-permute-start(bf16[256,512]{1,0:T(8,128)(2,1)} %bitcast.16), channel_id=1, source_target_pairs={{0,4},{2,6},{4,8},{6,10},{8,12},{10,14},{12,0},{14,2},{1,13},{3,15... | collective-permute-start | bytes 786440 | tf_op jit(solution)/shard_map/ppermute | solution.py:109
  10.7 16.7 %collective-permute-start.1 = (bf16[256,512]{1,0:T(8,128)(2,1)}, bf16[256,512]{1,0:T(8,128)(2,1)S(1)}, u32[]{:S(2)}, u32[]{:S(2)}) collective-permute-start(bf16[256,512]{1,0:T(8,128)(2,1)} %bitcast.17), channel_id=1, source_target_pairs={{0,12},{2,14},{4,0},{6,2},{8,4},{10,6},{12,8},{14,10},{1,5},{3,7},... | collective-permute-start | bytes 786440 | tf_op jit(solution)/shard_map/ppermute | solution.py:109
  15.0 14.4 %collective-permute-start.6 = (bf16[256,512]{1,0:T(8,128)(2,1)}, bf16[256,512]{1,0:T(8,128)(2,1)S(1)}, u32[]{:S(2)}, u32[]{:S(2)}) collective-permute-start(bf16[256,512]{1,0:T(8,128)(2,1)} %bitcast.18), channel_id=1, source_target_pairs={{0,14},{2,0},{4,2},{6,4},{8,6},{10,8},{12,10},{14,12},{1,3},{3,5},... | collective-permute-start | bytes 786440 | tf_op jit(solution)/shard_map/ppermute | solution.py:109
  17.0 0.7 copy-start.3
  17.8 14.9 %copy-start.4 = (s32[26]{0:T(128)}, s32[26]{0:T(128)S(1)}, u32[]{:S(2)}) copy-start(s32[26]{0:T(128)S(1)} %reshape.13.own) | copy-start | bytes 316
  17.8 4.5 %collective-permute-start = (s32[26]{0:T(128)S(1)}, s32[26]{0:T(128)S(1)}, u32[]{:S(2)}, u32[]{:S(2)}) collective-permute-start(s32[26]{0:T(128)S(1)} %reshape.13.own), channel_id=1, source_target_pairs={{0,1},{1,0},{2,3},{3,2},{4,5},{5,4},{6,7},{7,6},{8,9},{9,8},{10,11... | collective-permute-start | bytes 320 | tf_op jit(solution)/shard_map/ppermute | solution.py:113
  22.3 10.4 %copy-start.5 = (s32[26]{0:T(128)}, s32[26]{0:T(128)S(1)}, u32[]{:S(2)}) copy-start(s32[26]{0:T(128)S(1)} %collective-permute-done.partner) | copy-start | bytes 316
  22.3 12.0 %collective-permute-start.7 = (bf16[256,512]{1,0:T(8,128)(2,1)}, bf16[256,512]{1,0:T(8,128)(2,1)S(1)}, u32[]{:S(2)}, u32[]{:S(2)}) collective-permute-start(bf16[256,512]{1,0:T(8,128)(2,1)} %bitcast.19), channel_id=1, source_target_pairs={{0,2},{2,4},{4,6},{6,8},{8,10},{10,12},{12,14},{14,0},{1,15},{3,1}... | collective-permute-start | bytes 786440 | tf_op jit(solution)/shard_map/ppermute | solution.py:109
  25.5 12.0 %collective-permute-start.4 = (bf16[256,512]{1,0:T(8,128)(2,1)S(1)}, bf16[256,512]{1,0:T(8,128)(2,1)S(1)}, u32[]{:S(2)}, u32[]{:S(2)}) collective-permute-start(bf16[256,512]{1,0:T(8,128)(2,1)S(1)} %collective-permute-done.3.p6), channel_id=1, source_target_pairs={{0,4},{2,6},{4,8},{6,10},{8,12},{10,14},{12,0},{14,2},{1,13},{3,15... | collective-permute-start | bytes 786440 | tf_op jit(solution)/shard_map/ppermute | solution.py:109
  27.4 12.9 %collective-permute-start.5 = (bf16[256,512]{1,0:T(8,128)(2,1)S(1)}, bf16[256,512]{1,0:T(8,128)(2,1)S(1)}, u32[]{:S(2)}, u32[]{:S(2)}) collective-permute-start(bf16[256,512]{1,0:T(8,128)(2,1)S(1)} %collective-permute-done.3.p6), channel_id=1, source_target_pairs={{0,2},{2,4},{4,6},{6,8},{8,10},{10,12},{12,14},{14,0},{1,15},{3,1}... | collective-permute-start | bytes 786440 | tf_op jit(solution)/shard_map/ppermute | solution.py:109
  29.3 13.2 %collective-permute-start.2 = (bf16[256,512]{1,0:T(8,128)(2,1)S(1)}, bf16[256,512]{1,0:T(8,128)(2,1)S(1)}, u32[]{:S(2)}, u32[]{:S(2)}) collective-permute-start(bf16[256,512]{1,0:T(8,128)(2,1)S(1)} %collective-permute-done.1.p2), channel_id=1, source_target_pairs={{0,14},{2,0},{4,2},{6,4},{8,6},{10,8},{12,10},{14,12},{1,3},{3,5},... | collective-permute-start | bytes 786440 | tf_op jit(solution)/shard_map/ppermute | solution.py:109
  43.5 5.7 %collective-permute-start.9 = (f32[256,512]{1,0:T(8,128)S(1)}, f32[256,512]{1,0:T(8,128)S(1)}, u32[]{:S(2)}, u32[]{:S(2)}) collective-permute-start(f32[256,512]{1,0:T(8,128)S(1)} %shard_map.93), channel_id=1, source_target_pairs={{0,1},{1,0},{2,3},{3,2},{4,5},{5,4},{6,7},{7,6},{8,9},{9,8},{10,11... | collective-permute-start | bytes 1572872 | tf_op jit(solution)/shard_map/ppermute | solution.py:113
  47.5 1.6 %copy-start = (bf16[512,512]{1,0:T(8,128)(2,1)S(1)}, bf16[512,512]{1,0:T(8,128)(2,1)}, u32[]{:S(2)}) copy-start(bf16[512,512]{1,0:T(8,128)(2,1)} %w_message.2) | copy-start | bytes 1572868
  49.5 20.6 %copy-start.2 = (f32[16,512]{1,0:T(8,128)S(1)}, f32[16,512]{1,0:T(8,128)}, u32[]{:S(2)}) copy-start(f32[16,512]{1,0:T(8,128)} %taps.1) | copy-start | bytes 98308
  85.4 13.9 %collective-permute-start.10 = (bf16[256,512]{1,0:T(8,128)(2,1)S(1)}, bf16[256,512]{1,0:T(8,128)(2,1)S(1)}, u32[]{:S(2)}, u32[]{:S(2)}) collective-permute-start(bf16[256,512]{1,0:T(8,128)(2,1)S(1)} %bitcast.8), channel_id=1, source_target_pairs={{0,12},{2,14},{4,0},{6,2},{8,4},{10,6},{12,8},{14,10},{1,5},{3,7},... | collective-permute-start | bytes 786440 | tf_op jit(solution)/shard_map/ppermute | solution.py:109
  88.7 17.4 %collective-permute-start.12 = (bf16[256,512]{1,0:T(8,128)(2,1)S(1)}, bf16[256,512]{1,0:T(8,128)(2,1)S(1)}, u32[]{:S(2)}, u32[]{:S(2)}) collective-permute-start(bf16[256,512]{1,0:T(8,128)(2,1)S(1)} %bitcast.9), channel_id=1, source_target_pairs={{0,4},{2,6},{4,8},{6,10},{8,12},{10,14},{12,0},{14,2},{1,13},{3,15... | collective-permute-start | bytes 786440 | tf_op jit(solution)/shard_map/ppermute | solution.py:109
  92.8 19.4 %collective-permute-start.15 = (bf16[256,512]{1,0:T(8,128)(2,1)S(1)}, bf16[256,512]{1,0:T(8,128)(2,1)S(1)}, u32[]{:S(2)}, u32[]{:S(2)}) collective-permute-start(bf16[256,512]{1,0:T(8,128)(2,1)S(1)} %bitcast.10), channel_id=1, source_target_pairs={{0,14},{2,0},{4,2},{6,4},{8,6},{10,8},{12,10},{14,12},{1,3},{3,5},... | collective-permute-start | bytes 786440 | tf_op jit(solution)/shard_map/ppermute | solution.py:109
  94.9 17.2 %collective-permute-start.16 = (bf16[256,512]{1,0:T(8,128)(2,1)S(1)}, bf16[256,512]{1,0:T(8,128)(2,1)S(1)}, u32[]{:S(2)}, u32[]{:S(2)}) collective-permute-start(bf16[256,512]{1,0:T(8,128)(2,1)S(1)} %bitcast.11), channel_id=1, source_target_pairs={{0,2},{2,4},{4,6},{6,8},{8,10},{10,12},{12,14},{14,0},{1,15},{3,1}... | collective-permute-start | bytes 786440 | tf_op jit(solution)/shard_map/ppermute | solution.py:109
  99.3 15.2 %collective-permute-start.11 = (bf16[256,512]{1,0:T(8,128)(2,1)S(1)}, bf16[256,512]{1,0:T(8,128)(2,1)S(1)}, u32[]{:S(2)}, u32[]{:S(2)}) collective-permute-start(bf16[256,512]{1,0:T(8,128)(2,1)S(1)} %collective-permute-done.10.p2), channel_id=1, source_target_pairs={{0,14},{2,0},{4,2},{6,4},{8,6},{10,8},{12,10},{14,12},{1,3},{3,5},... | collective-permute-start | bytes 786440 | tf_op jit(solution)/shard_map/ppermute | solution.py:109
  106.1 14.0 %collective-permute-start.13 = (bf16[256,512]{1,0:T(8,128)(2,1)S(1)}, bf16[256,512]{1,0:T(8,128)(2,1)S(1)}, u32[]{:S(2)}, u32[]{:S(2)}) collective-permute-start(bf16[256,512]{1,0:T(8,128)(2,1)S(1)} %collective-permute-done.12.p6), channel_id=1, source_target_pairs={{0,4},{2,6},{4,8},{6,10},{8,12},{10,14},{12,0},{14,2},{1,13},{3,15... | collective-permute-start | bytes 786440 | tf_op jit(solution)/shard_map/ppermute | solution.py:109
  110.2 12.2 %collective-permute-start.14 = (bf16[256,512]{1,0:T(8,128)(2,1)S(1)}, bf16[256,512]{1,0:T(8,128)(2,1)S(1)}, u32[]{:S(2)}, u32[]{:S(2)}) collective-permute-start(bf16[256,512]{1,0:T(8,128)(2,1)S(1)} %collective-permute-done.12.p6), channel_id=1, source_target_pairs={{0,2},{2,4},{4,6},{6,8},{8,10},{10,12},{12,14},{14,0},{1,15},{3,1}... | collective-permute-start | bytes 786440 | tf_op jit(solution)/shard_map/ppermute | solution.py:109
  123.3 7.8 %collective-permute-start.17 = (f32[256,512]{1,0:T(8,128)S(1)}, f32[256,512]{1,0:T(8,128)S(1)}, u32[]{:S(2)}, u32[]{:S(2)}) collective-permute-start(f32[256,512]{1,0:T(8,128)S(1)} %shard_map.98), channel_id=1, source_target_pairs={{0,1},{1,0},{2,3},{3,2},{4,5},{5,4},{6,7},{7,6},{8,9},{9,8},{10,11... | collective-permute-start | bytes 1572872 | tf_op jit(solution)/shard_map/ppermute | solution.py:113
  129.5 1.6 %copy-start.1 = (bf16[512,512]{1,0:T(8,128)(2,1)S(1)}, bf16[512,512]{1,0:T(8,128)(2,1)}, u32[]{:S(2)}) copy-start(bf16[512,512]{1,0:T(8,128)(2,1)} %w_message.3) | copy-start | bytes 1572868

commit v4 on v3

--- a/solution.py
+++ b/solution.py
@@ -97,8 +97,10 @@
 
 
 def last_kernel(mine, received, root, w_message, out):
-    total = (mine[...] + received[...]).astype(jnp.bfloat16)
-    full = jnp.dot(total, w_message[...], preferred_element_type=jnp.float32) + root[...]
+    size = out.shape[0]
+    rows = pl.ds(pl.multiple_of(pl.program_id(0) * size, size), size)
+    total = (mine[rows, :] + received[rows, :]).astype(jnp.bfloat16)
+    full = jnp.dot(total, w_message[...], preferred_element_type=jnp.float32) + root[rows, :]
     out[...] = jnp.maximum(full, 0.0).astype(jnp.bfloat16)
 
 
@@ -164,14 +166,17 @@
 
     received = swap(finish(1, other_tiles, theirs))
     mine = finish(0, own_tiles, mine)
-    out = call(
+    blocks = 1 if fetch else 2
+    out = pl.pallas_call(
         last_kernel,
-        jax.ShapeDtypeStruct((rows, width), jnp.bfloat16),
-        (mine, received, root, w_message),
-        [VMEM] * 4,
-        dense,
-        14 * area,
-    )
+        out_shape=jax.ShapeDtypeStruct((rows, width), jnp.bfloat16),
+        grid=(blocks,),
+        in_specs=[VMEM] * 4,
+        out_specs=pl.BlockSpec((rows // blocks, width), lambda i: (i, 0)),
+        cost_estimate=pl.CostEstimate(flops=dense, bytes_accessed=14 * area, transcendentals=0),
+        compiler_params=pltpu.CompilerParams(vmem_limit_bytes=16 << 20),
+        name="last",
+    )(mine, received, root, w_message)
     return out, own_tiles
 
 

time: 133 us -> 133 us (level)
    pallas_call x0 -> x2, Pallas kernels: none -> 1.47 us  [graph_layer(): pl.pallas_call(last_kernel, out_shape=jax.ShapeDtypeStruct((rows, width),...]
    pallas_call x9 -> x7, Pallas kernels: 11.9 us -> 10.6 us  [call(): pl.pallas_call(kernel, out_shape=outs, in_specs=specs, out_specs=jax.tree...]
where the time goes in v4:
time: 133 us; the launch traced here: 132 us
  starting transfers between devices  62.8 us (47%)
  blocking collectives  35.3 us (27%)
  waiting for transfers between devices  19.2 us (14%)
  Pallas kernels  13.6 us (10%)
    ppermute x14, starting transfers between devices, shift(): return lax.ppermute(x, 'vert', pairs)  40.2 us
    ppermute x4, starting transfers between devices, swap(): return lax.ppermute(x, 'vert', [(v, v ^ 1) for v in range(2 * RING)])  22.6 us
    all_to_all x1, blocking collectives, temporal(): by_vertex = lax.all_to_all(split, 'snap', split_axis=0, concat_axis=0)  20.6 us
    ppermute x14, waiting for transfers between devices, shift(): return lax.ppermute(x, 'vert', pairs)  18.4 us
    all_to_all x1, blocking collectives, temporal(): returned = lax.all_to_all(mixed, 'snap', split_axis=0, concat_axis=0)  14.7 us
    pallas_call x7, Pallas kernels, call(): pl.pallas_call(kernel, out_shape=outs, in_specs=specs, out_specs=jax.tree...  10.6 us
  transfers between devices with their start and end apart: 18, of which 7 were waited for; matrix products, arithmetic and copies ran while one was open for 0% of the time, Pallas kernels for 7%

profile of v4, /device:TPU:1, one launch (start us, length us, event | category | flops | bytes accessed | tf_op | source)
XLA Modules:
  0.0 132.3 jit_solution(12685389979040476610)
XLA Ops:
  0.0 8.7 %collective-permute-start.8 = (bf16[24,128,128]{2,1,0:T(8,128)(2,1)}, bf16[24,128,128]{2,1,0:T(8,128)(2,1)S(1)}, u32[]{:S(2)}, u32[]{:S(2)}) collective-permute-start(bf16[24,128,128]{2,1,0:T(8,128)(2,1)} %bitcast.14), channel_id=1, source_target_pairs={{0,1},{1,0},{2,3},{3,2},{4,5},{5,4},{6,7},{7,6},{8,9},{9,8},{10,11... | collective-permute-start | bytes 2359304 | tf_op jit(solution)/shard_map/ppermute | solution.py:115
  8.7 0.0 copy-start.6
  8.8 1.9 %collective-permute-start.3 = (bf16[256,512]{1,0:T(8,128)(2,1)}, bf16[256,512]{1,0:T(8,128)(2,1)S(1)}, u32[]{:S(2)}, u32[]{:S(2)}) collective-permute-start(bf16[256,512]{1,0:T(8,128)(2,1)} %bitcast.16), channel_id=1, source_target_pairs={{0,4},{2,6},{4,8},{6,10},{8,12},{10,14},{12,0},{14,2},{1,13},{3,15... | collective-permute-start | bytes 786440 | tf_op jit(solution)/shard_map/ppermute | solution.py:111
  10.7 4.3 %collective-permute-start.1 = (bf16[256,512]{1,0:T(8,128)(2,1)}, bf16[256,512]{1,0:T(8,128)(2,1)S(1)}, u32[]{:S(2)}, u32[]{:S(2)}) collective-permute-start(bf16[256,512]{1,0:T(8,128)(2,1)} %bitcast.17), channel_id=1, source_target_pairs={{0,12},{2,14},{4,0},{6,2},{8,4},{10,6},{12,8},{14,10},{1,5},{3,7},... | collective-permute-start | bytes 786440 | tf_op jit(solution)/shard_map/ppermute | solution.py:111
  15.0 1.9 %collective-permute-start.6 = (bf16[256,512]{1,0:T(8,128)(2,1)}, bf16[256,512]{1,0:T(8,128)(2,1)S(1)}, u32[]{:S(2)}, u32[]{:S(2)}) collective-permute-start(bf16[256,512]{1,0:T(8,128)(2,1)} %bitcast.18), channel_id=1, source_target_pairs={{0,14},{2,0},{4,2},{6,4},{8,6},{10,8},{12,10},{14,12},{1,3},{3,5},... | collective-permute-start | bytes 786440 | tf_op jit(solution)/shard_map/ppermute | solution.py:111
  16.9 0.0 copy-done.6
  16.9 0.1 copy.14
  17.0 0.0 copy-start.3
  17.0 0.7 copy-done.3
  17.7 0.1 pad_add_fusion
  17.7 0.1 reshape.13.own
  17.8 3.7 %collective-permute-start = (s32[26]{0:T(128)S(1)}, s32[26]{0:T(128)S(1)}, u32[]{:S(2)}, u32[]{:S(2)}) collective-permute-start(s32[26]{0:T(128)S(1)} %reshape.13.own), channel_id=1, source_target_pairs={{0,1},{1,0},{2,3},{3,2},{4,5},{5,4},{6,7},{7,6},{8,9},{9,8},{10,11... | collective-permute-start | bytes 320 | tf_op jit(solution)/shard_map/ppermute | solution.py:115
  21.5 0.8 collective-permute-done.partner
  22.3 0.0 copy-start.5
  22.3 3.1 %collective-permute-start.7 = (bf16[256,512]{1,0:T(8,128)(2,1)}, bf16[256,512]{1,0:T(8,128)(2,1)S(1)}, u32[]{:S(2)}, u32[]{:S(2)}) collective-permute-start(bf16[256,512]{1,0:T(8,128)(2,1)} %bitcast.19), channel_id=1, source_target_pairs={{0,2},{2,4},{4,6},{6,8},{8,10},{10,12},{12,14},{14,0},{1,15},{3,1}... | collective-permute-start | bytes 786440 | tf_op jit(solution)/shard_map/ppermute | solution.py:111
  25.4 0.0 collective-permute-done.3.p6
  25.5 1.9 %collective-permute-start.4 = (bf16[256,512]{1,0:T(8,128)(2,1)S(1)}, bf16[256,512]{1,0:T(8,128)(2,1)S(1)}, u32[]{:S(2)}, u32[]{:S(2)}) collective-permute-start(bf16[256,512]{1,0:T(8,128)(2,1)S(1)} %collective-permute-done.3.p6), channel_id=1, source_target_pairs={{0,4},{2,6},{4,8},{6,10},{8,12},{10,14},{12,0},{14,2},{1,13},{3,15... | collective-permute-start | bytes 786440 | tf_op jit(solution)/shard_map/ppermute | solution.py:111
  27.4 0.0 collective-permute-done.1.p2
  27.4 1.9 %collective-permute-start.5 = (bf16[256,512]{1,0:T(8,128)(2,1)S(1)}, bf16[256,512]{1,0:T(8,128)(2,1)S(1)}, u32[]{:S(2)}, u32[]{:S(2)}) collective-permute-start(bf16[256,512]{1,0:T(8,128)(2,1)S(1)} %collective-permute-done.3.p6), channel_id=1, source_target_pairs={{0,2},{2,4},{4,6},{6,8},{8,10},{10,12},{12,14},{14,0},{1,15},{3,1}... | collective-permute-start | bytes 786440 | tf_op jit(solution)/shard_map/ppermute | solution.py:111
  29.3 0.0 collective-permute-done.6.p1
  29.3 3.4 %collective-permute-start.2 = (bf16[256,512]{1,0:T(8,128)(2,1)S(1)}, bf16[256,512]{1,0:T(8,128)(2,1)S(1)}, u32[]{:S(2)}, u32[]{:S(2)}) collective-permute-start(bf16[256,512]{1,0:T(8,128)(2,1)S(1)} %collective-permute-done.1.p2), channel_id=1, source_target_pairs={{0,14},{2,0},{4,2},{6,4},{8,6},{10,8},{12,10},{14,12},{1,3},{3,5},... | collective-permute-start | bytes 786440 | tf_op jit(solution)/shard_map/ppermute | solution.py:111
  32.7 0.0 copy-done.4
  32.7 0.0 copy-done.5
  32.7 1.6 %plan.1 = s32[400]{0:T(512)} custom-call(s32[1]{0:T(128)} %bitcast.where, s32[26]{0:T(128)} %copy-done.4, s32[26]{0:T(128)} %copy-done.5), custom_call_target="tpu_custom_call" | custom-call | flops 1000 | bytes 4000 | tf_op jit(solution)/shard_map/plan/pallas_call | solution.py:225
  34.3 0.0 collective-permute-done.7.p7
  34.3 0.0 collective-permute-done.8.other_tiles.tiles
  34.3 2.6 %shard_map.91 = (f32[256,512]{1,0:T(8,128)S(1)}, f32[256,512]{1,0:T(8,128)S(1)}, f32[256,512]{1,0:T(8,128)S(1)}, bf16[24,128,128]{2,1,0:T(8,128)(2,1)S(1)}) custom-call(s32[400]{0:T(512)} %plan.1, bf16[256,512]{1,0:T(8,128)(2,1)} %bitcast.20, bf16[256,512]{1,0:T(8,128)(2,1)S(1)} %collective-permute-done.6.p1, ...), custom_call_target="tpu_custom_call" | custom-call | flops 536870912 | bytes 3145728 | tf_op jit(solution)/shard_map/pallas_call | solution.py:19
  37.0 0.5 collective-permute-done.4.p4
  37.5 2.8 %collective-permute-done.5.p5 = bf16[256,512]{1,0:T(8,128)(2,1)S(1)} collective-permute-done((bf16[256,512]{1,0:T(8,128)(2,1)S(1)}, bf16[256,512]{1,0:T(8,128)(2,1)S(1)}, u32[]{:S(2)}, u32[]{:S(2)}) %collective-permute-start.5) | collective-permute-done | bytes 262176 | tf_op jit(solution)/shard_map/ppermute | solution.py:111
  40.3 2.3 %collective-permute-done.2.p3 = bf16[256,512]{1,0:T(8,128)(2,1)S(1)} collective-permute-done((bf16[256,512]{1,0:T(8,128)(2,1)S(1)}, bf16[256,512]{1,0:T(8,128)(2,1)S(1)}, u32[]{:S(2)}, u32[]{:S(2)}) %collective-permute-start.2) | collective-permute-done | bytes 262176 | tf_op jit(solution)/shard_map/ppermute | solution.py:111
  42.5 0.9 shard_map.93
  43.5 4.0 %collective-permute-start.9 = (f32[256,512]{1,0:T(8,128)S(1)}, f32[256,512]{1,0:T(8,128)S(1)}, u32[]{:S(2)}, u32[]{:S(2)}) collective-permute-start(f32[256,512]{1,0:T(8,128)S(1)} %shard_map.93), channel_id=1, source_target_pairs={{0,1},{1,0},{2,3},{3,2},{4,5},{5,4},{6,7},{7,6},{8,9},{9,8},{10,11... | collective-permute-start | bytes 1572872 | tf_op jit(solution)/shard_map/ppermute | solution.py:115
  47.5 0.0 copy-start
  47.5 1.6 %shard_map.92.mine = f32[256,512]{1,0:T(8,128)S(1)} custom-call(s32[400]{0:T(512)} %plan.1, bf16[256,512]{1,0:T(8,128)(2,1)S(1)} %collective-permute-done.2.p3, bf16[256,512]{1,0:T(8,128)(2,1)S(1)} %collective-permute-done.4.p4, bf16[256,512]{1,0:T(8,128)(2,1)S(1)} %collective-permute-done.5.p5, ...), custom_call_target="tpu_custom_call", output_to_operand_aliasing={{}: (5, {})} | custom-call | flops 134217728 | bytes 1048576 | tf_op jit(solution)/shard_map/pallas_call | solution.py:19
  49.1 0.0 collective-permute-done.9.received
  49.2 0.0 copy-done
  49.2 0.3 last.2
  49.5 0.0 copy-start.2
  49.5 20.6 %all_to_all.10.hidden = bf16[32,8,512]{2,1,0:T(8,128)(2,1)S(1)} all-to-all(bf16[32,8,512]{2,1,0:T(8,128)(2,1)S(1)} %bitcast.13), channel_id=1, replica_groups=mesh['snap'=32,'vert'=16] {'snap'}, dimensions={0} | all-to-all | bytes 524288 | tf_op jit(solution)/shard_map/all_to_all | solution.py:196
  70.0 0.0 copy-done.2
  70.1 0.6 shard_map.94
  70.6 14.7 %all_to_all.11 = bf16[32,8,512]{2,1,0:T(8,128)(2,1)S(1)} all-to-all(bf16[32,8,512]{2,1,0:T(8,128)(2,1)S(1)} %shard_map.94), channel_id=1, replica_groups=mesh['snap'=32,'vert'=16] {'snap'}, dimensions={0} | all-to-all | bytes 524288 | tf_op jit(solution)/shard_map/all_to_all | solution.py:205
  85.4 3.3 %collective-permute-start.10 = (bf16[256,512]{1,0:T(8,128)(2,1)S(1)}, bf16[256,512]{1,0:T(8,128)(2,1)S(1)}, u32[]{:S(2)}, u32[]{:S(2)}) collective-permute-start(bf16[256,512]{1,0:T(8,128)(2,1)S(1)} %bitcast.8), channel_id=1, source_target_pairs={{0,12},{2,14},{4,0},{6,2},{8,4},{10,6},{12,8},{14,10},{1,5},{3,7},... | collective-permute-start | bytes 786440 | tf_op jit(solution)/shard_map/ppermute | solution.py:111
  88.7 4.1 %collective-permute-start.12 = (bf16[256,512]{1,0:T(8,128)(2,1)S(1)}, bf16[256,512]{1,0:T(8,128)(2,1)S(1)}, u32[]{:S(2)}, u32[]{:S(2)}) collective-permute-start(bf16[256,512]{1,0:T(8,128)(2,1)S(1)} %bitcast.9), channel_id=1, source_target_pairs={{0,4},{2,6},{4,8},{6,10},{8,12},{10,14},{12,0},{14,2},{1,13},{3,15... | collective-permute-start | bytes 786440 | tf_op jit(solution)/shard_map/ppermute | solution.py:111
  92.8 2.2 %collective-permute-start.15 = (bf16[256,512]{1,0:T(8,128)(2,1)S(1)}, bf16[256,512]{1,0:T(8,128)(2,1)S(1)}, u32[]{:S(2)}, u32[]{:S(2)}) collective-permute-start(bf16[256,512]{1,0:T(8,128)(2,1)S(1)} %bitcast.10), channel_id=1, source_target_pairs={{0,14},{2,0},{4,2},{6,4},{8,6},{10,8},{12,10},{14,12},{1,3},{3,5},... | collective-permute-start | bytes 786440 | tf_op jit(solution)/shard_map/ppermute | solution.py:111
  94.9 4.3 %collective-permute-start.16 = (bf16[256,512]{1,0:T(8,128)(2,1)S(1)}, bf16[256,512]{1,0:T(8,128)(2,1)S(1)}, u32[]{:S(2)}, u32[]{:S(2)}) collective-permute-start(bf16[256,512]{1,0:T(8,128)(2,1)S(1)} %bitcast.11), channel_id=1, source_target_pairs={{0,2},{2,4},{4,6},{6,8},{8,10},{10,12},{12,14},{14,0},{1,15},{3,1}... | collective-permute-start | bytes 786440 | tf_op jit(solution)/shard_map/ppermute | solution.py:111
  99.3 0.0 collective-permute-done.10.p2
  99.3 1.9 %collective-permute-start.11 = (bf16[256,512]{1,0:T(8,128)(2,1)S(1)}, bf16[256,512]{1,0:T(8,128)(2,1)S(1)}, u32[]{:S(2)}, u32[]{:S(2)}) collective-permute-start(bf16[256,512]{1,0:T(8,128)(2,1)S(1)} %collective-permute-done.10.p2), channel_id=1, source_target_pairs={{0,14},{2,0},{4,2},{6,4},{8,6},{10,8},{12,10},{14,12},{1,3},{3,5},... | collective-permute-start | bytes 786440 | tf_op jit(solution)/shard_map/ppermute | solution.py:111
  101.2 4.9 %collective-permute-done.12.p6 = bf16[256,512]{1,0:T(8,128)(2,1)S(1)} collective-permute-done((bf16[256,512]{1,0:T(8,128)(2,1)S(1)}, bf16[256,512]{1,0:T(8,128)(2,1)S(1)}, u32[]{:S(2)}, u32[]{:S(2)}) %collective-permute-start.12) | collective-permute-done | bytes 262176 | tf_op jit(solution)/shard_map/ppermute | solution.py:111
  106.1 4.1 %collective-permute-start.13 = (bf16[256,512]{1,0:T(8,128)(2,1)S(1)}, bf16[256,512]{1,0:T(8,128)(2,1)S(1)}, u32[]{:S(2)}, u32[]{:S(2)}) collective-permute-start(bf16[256,512]{1,0:T(8,128)(2,1)S(1)} %collective-permute-done.12.p6), channel_id=1, source_target_pairs={{0,4},{2,6},{4,8},{6,10},{8,12},{10,14},{12,0},{14,2},{1,13},{3,15... | collective-permute-start | bytes 786440 | tf_op jit(solution)/shard_map/ppermute | solution.py:111
  110.2 1.9 %collective-permute-start.14 = (bf16[256,512]{1,0:T(8,128)(2,1)S(1)}, bf16[256,512]{1,0:T(8,128)(2,1)S(1)}, u32[]{:S(2)}, u32[]{:S(2)}) collective-permute-start(bf16[256,512]{1,0:T(8,128)(2,1)S(1)} %collective-permute-done.12.p6), channel_id=1, source_target_pairs={{0,2},{2,4},{4,6},{6,8},{8,10},{10,12},{12,14},{14,0},{1,15},{3,1}... | collective-permute-start | bytes 786440 | tf_op jit(solution)/shard_map/ppermute | solution.py:111
  112.1 0.0 collective-permute-done.15.p1
  112.1 0.0 collective-permute-done.16.p7
  112.2 2.3 %shard_map.95 = (f32[256,512]{1,0:T(8,128)S(1)}, f32[256,512]{1,0:T(8,128)S(1)}, f32[256,512]{1,0:T(8,128)S(1)}) custom-call(s32[400]{0:T(512)} %plan.1, bf16[256,512]{1,0:T(8,128)(2,1)S(1)} %bitcast.12, bf16[256,512]{1,0:T(8,128)(2,1)S(1)} %collective-permute-done.15.p1, bf16[256,512]{1,0:T(8,128)(2,1)S(1)} %collective-permute-done.10.p2, ...), custom_call_target="tpu_custom_call" | custom-call | flops 536870912 | bytes 3145728 | tf_op jit(solution)/shard_map/pallas_call | solution.py:19
  114.4 0.0 collective-permute-done.11.p3
  114.5 5.7 %collective-permute-done.13.p4 = bf16[256,512]{1,0:T(8,128)(2,1)S(1)} collective-permute-done((bf16[256,512]{1,0:T(8,128)(2,1)S(1)}, bf16[256,512]{1,0:T(8,128)(2,1)S(1)}, u32[]{:S(2)}, u32[]{:S(2)}) %collective-permute-start.13) | collective-permute-done | bytes 262176 | tf_op jit(solution)/shard_map/ppermute | solution.py:111
  120.2 2.2 %collective-permute-done.14.p5 = bf16[256,512]{1,0:T(8,128)(2,1)S(1)} collective-permute-done((bf16[256,512]{1,0:T(8,128)(2,1)S(1)}, bf16[256,512]{1,0:T(8,128)(2,1)S(1)}, u32[]{:S(2)}, u32[]{:S(2)}) %collective-permute-start.14) | collective-permute-done | bytes 262176 | tf_op jit(solution)/shard_map/ppermute | solution.py:111
  122.4 1.0 shard_map.97
  123.3 6.1 %collective-permute-start.17 = (f32[256,512]{1,0:T(8,128)S(1)}, f32[256,512]{1,0:T(8,128)S(1)}, u32[]{:S(2)}, u32[]{:S(2)}) collective-permute-start(f32[256,512]{1,0:T(8,128)S(1)} %shard_map.97), channel_id=1, source_target_pairs={{0,1},{1,0},{2,3},{3,2},{4,5},{5,4},{6,7},{7,6},{8,9},{9,8},{10,11... | collective-permute-start | bytes 1572872 | tf_op jit(solution)/shard_map/ppermute | solution.py:115
  129.5 0.0 copy-start.1
  129.5 1.6 %shard_map.96.mine = f32[256,512]{1,0:T(8,128)S(1)} custom-call(s32[400]{0:T(512)} %plan.1, bf16[256,512]{1,0:T(8,128)(2,1)S(1)} %collective-permute-done.11.p3, bf16[256,512]{1,0:T(8,128)(2,1)S(1)} %collective-permute-done.13.p4, bf16[256,512]{1,0:T(8,128)(2,1)S(1)} %collective-permute-done.14.p5, ...), custom_call_target="tpu_custom_call", output_to_operand_aliasing={{}: (5, {})} | custom-call | flops 134217728 | bytes 1048576 | tf_op jit(solution)/shard_map/pallas_call | solution.py:19
  131.1 0.0 collective-permute-done.17.received
  131.1 0.0 copy-done.1
  131.1 1.2 last.3
  (1 shorter events, 0.0 us)
Async XLA Ops:
  0.0 34.3 %collective-permute-start.8 = (bf16[24,128,128]{2,1,0:T(8,128)(2,1)}, bf16[24,128,128]{2,1,0:T(8,128)(2,1)S(1)}, u32[]{:S(2)}, u32[]{:S(2)}) collective-permute-start(bf16[24,128,128]{2,1,0:T(8,128)(2,1)} %bitcast.14), channel_id=1, source_target_pairs={{0,1},{1,0},{2,3},{3,2},{4,5},{5,4},{6,7},{7,6},{8,9},{9,8},{10,11... | collective-permute-start | bytes 2359304 | tf_op jit(solution)/shard_map/ppermute | solution.py:115
  8.7 8.1 %copy-start.6 = (s32[1,2]{1,0:T(1,128)S(1)}, s32[1,2]{1,0:T(1,128)}, u32[]{:S(2)}) copy-start(s32[1,2]{1,0:T(1,128)} %param.12) | copy-start | bytes 28
  8.8 16.7 %collective-permute-start.3 = (bf16[256,512]{1,0:T(8,128)(2,1)}, bf16[256,512]{1,0:T(8,128)(2,1)S(1)}, u32[]{:S(2)}, u32[]{:S(2)}) collective-permute-start(bf16[256,512]{1,0:T(8,128)(2,1)} %bitcast.16), channel_id=1, source_target_pairs={{0,4},{2,6},{4,8},{6,10},{8,12},{10,14},{12,0},{14,2},{1,13},{3,15... | collective-permute-start | bytes 786440 | tf_op jit(solution)/shard_map/ppermute | solution.py:111
  10.7 16.7 %collective-permute-start.1 = (bf16[256,512]{1,0:T(8,128)(2,1)}, bf16[256,512]{1,0:T(8,128)(2,1)S(1)}, u32[]{:S(2)}, u32[]{:S(2)}) collective-permute-start(bf16[256,512]{1,0:T(8,128)(2,1)} %bitcast.17), channel_id=1, source_target_pairs={{0,12},{2,14},{4,0},{6,2},{8,4},{10,6},{12,8},{14,10},{1,5},{3,7},... | collective-permute-start | bytes 786440 | tf_op jit(solution)/shard_map/ppermute | solution.py:111
  15.0 14.4 %collective-permute-start.6 = (bf16[256,512]{1,0:T(8,128)(2,1)}, bf16[256,512]{1,0:T(8,128)(2,1)S(1)}, u32[]{:S(2)}, u32[]{:S(2)}) collective-permute-start(bf16[256,512]{1,0:T(8,128)(2,1)} %bitcast.18), channel_id=1, source_target_pairs={{0,14},{2,0},{4,2},{6,4},{8,6},{10,8},{12,10},{14,12},{1,3},{3,5},... | collective-permute-start | bytes 786440 | tf_op jit(solution)/shard_map/ppermute | solution.py:111
  17.0 0.7 copy-start.3
  17.8 14.9 %copy-start.4 = (s32[26]{0:T(128)}, s32[26]{0:T(128)S(1)}, u32[]{:S(2)}) copy-start(s32[26]{0:T(128)S(1)} %reshape.13.own) | copy-start | bytes 316
  17.8 4.5 %collective-permute-start = (s32[26]{0:T(128)S(1)}, s32[26]{0:T(128)S(1)}, u32[]{:S(2)}, u32[]{:S(2)}) collective-permute-start(s32[26]{0:T(128)S(1)} %reshape.13.own), channel_id=1, source_target_pairs={{0,1},{1,0},{2,3},{3,2},{4,5},{5,4},{6,7},{7,6},{8,9},{9,8},{10,11... | collective-permute-start | bytes 320 | tf_op jit(solution)/shard_map/ppermute | solution.py:115
  22.3 10.4 %copy-start.5 = (s32[26]{0:T(128)}, s32[26]{0:T(128)S(1)}, u32[]{:S(2)}) copy-start(s32[26]{0:T(128)S(1)} %collective-permute-done.partner) | copy-start | bytes 316
  22.3 12.0 %collective-permute-start.7 = (bf16[256,512]{1,0:T(8,128)(2,1)}, bf16[256,512]{1,0:T(8,128)(2,1)S(1)}, u32[]{:S(2)}, u32[]{:S(2)}) collective-permute-start(bf16[256,512]{1,0:T(8,128)(2,1)} %bitcast.19), channel_id=1, source_target_pairs={{0,2},{2,4},{4,6},{6,8},{8,10},{10,12},{12,14},{14,0},{1,15},{3,1}... | collective-permute-start | bytes 786440 | tf_op jit(solution)/shard_map/ppermute | solution.py:111
  25.5 12.0 %collective-permute-start.4 = (bf16[256,512]{1,0:T(8,128)(2,1)S(1)}, bf16[256,512]{1,0:T(8,128)(2,1)S(1)}, u32[]{:S(2)}, u32[]{:S(2)}) collective-permute-start(bf16[256,512]{1,0:T(8,128)(2,1)S(1)} %collective-permute-done.3.p6), channel_id=1, source_target_pairs={{0,4},{2,6},{4,8},{6,10},{8,12},{10,14},{12,0},{14,2},{1,13},{3,15... | collective-permute-start | bytes 786440 | tf_op jit(solution)/shard_map/ppermute | solution.py:111
  27.4 12.9 %collective-permute-start.5 = (bf16[256,512]{1,0:T(8,128)(2,1)S(1)}, bf16[256,512]{1,0:T(8,128)(2,1)S(1)}, u32[]{:S(2)}, u32[]{:S(2)}) collective-permute-start(bf16[256,512]{1,0:T(8,128)(2,1)S(1)} %collective-permute-done.3.p6), channel_id=1, source_target_pairs={{0,2},{2,4},{4,6},{6,8},{8,10},{10,12},{12,14},{14,0},{1,15},{3,1}... | collective-permute-start | bytes 786440 | tf_op jit(solution)/shard_map/ppermute | solution.py:111
  29.3 13.2 %collective-permute-start.2 = (bf16[256,512]{1,0:T(8,128)(2,1)S(1)}, bf16[256,512]{1,0:T(8,128)(2,1)S(1)}, u32[]{:S(2)}, u32[]{:S(2)}) collective-permute-start(bf16[256,512]{1,0:T(8,128)(2,1)S(1)} %collective-permute-done.1.p2), channel_id=1, source_target_pairs={{0,14},{2,0},{4,2},{6,4},{8,6},{10,8},{12,10},{14,12},{1,3},{3,5},... | collective-permute-start | bytes 786440 | tf_op jit(solution)/shard_map/ppermute | solution.py:111
  43.5 5.7 %collective-permute-start.9 = (f32[256,512]{1,0:T(8,128)S(1)}, f32[256,512]{1,0:T(8,128)S(1)}, u32[]{:S(2)}, u32[]{:S(2)}) collective-permute-start(f32[256,512]{1,0:T(8,128)S(1)} %shard_map.93), channel_id=1, source_target_pairs={{0,1},{1,0},{2,3},{3,2},{4,5},{5,4},{6,7},{7,6},{8,9},{9,8},{10,11... | collective-permute-start | bytes 1572872 | tf_op jit(solution)/shard_map/ppermute | solution.py:115
  47.5 1.6 %copy-start = (bf16[512,512]{1,0:T(8,128)(2,1)S(1)}, bf16[512,512]{1,0:T(8,128)(2,1)}, u32[]{:S(2)}) copy-start(bf16[512,512]{1,0:T(8,128)(2,1)} %w_message.2) | copy-start | bytes 1572868
  49.5 20.6 %copy-start.2 = (f32[16,512]{1,0:T(8,128)S(1)}, f32[16,512]{1,0:T(8,128)}, u32[]{:S(2)}) copy-start(f32[16,512]{1,0:T(8,128)} %taps.1) | copy-start | bytes 98308
  85.4 13.9 %collective-permute-start.10 = (bf16[256,512]{1,0:T(8,128)(2,1)S(1)}, bf16[256,512]{1,0:T(8,128)(2,1)S(1)}, u32[]{:S(2)}, u32[]{:S(2)}) collective-permute-start(bf16[256,512]{1,0:T(8,128)(2,1)S(1)} %bitcast.8), channel_id=1, source_target_pairs={{0,12},{2,14},{4,0},{6,2},{8,4},{10,6},{12,8},{14,10},{1,5},{3,7},... | collective-permute-start | bytes 786440 | tf_op jit(solution)/shard_map/ppermute | solution.py:111
  88.7 17.4 %collective-permute-start.12 = (bf16[256,512]{1,0:T(8,128)(2,1)S(1)}, bf16[256,512]{1,0:T(8,128)(2,1)S(1)}, u32[]{:S(2)}, u32[]{:S(2)}) collective-permute-start(bf16[256,512]{1,0:T(8,128)(2,1)S(1)} %bitcast.9), channel_id=1, source_target_pairs={{0,4},{2,6},{4,8},{6,10},{8,12},{10,14},{12,0},{14,2},{1,13},{3,15... | collective-permute-start | bytes 786440 | tf_op jit(solution)/shard_map/ppermute | solution.py:111
  92.8 19.4 %collective-permute-start.15 = (bf16[256,512]{1,0:T(8,128)(2,1)S(1)}, bf16[256,512]{1,0:T(8,128)(2,1)S(1)}, u32[]{:S(2)}, u32[]{:S(2)}) collective-permute-start(bf16[256,512]{1,0:T(8,128)(2,1)S(1)} %bitcast.10), channel_id=1, source_target_pairs={{0,14},{2,0},{4,2},{6,4},{8,6},{10,8},{12,10},{14,12},{1,3},{3,5},... | collective-permute-start | bytes 786440 | tf_op jit(solution)/shard_map/ppermute | solution.py:111
  94.9 17.2 %collective-permute-start.16 = (bf16[256,512]{1,0:T(8,128)(2,1)S(1)}, bf16[256,512]{1,0:T(8,128)(2,1)S(1)}, u32[]{:S(2)}, u32[]{:S(2)}) collective-permute-start(bf16[256,512]{1,0:T(8,128)(2,1)S(1)} %bitcast.11), channel_id=1, source_target_pairs={{0,2},{2,4},{4,6},{6,8},{8,10},{10,12},{12,14},{14,0},{1,15},{3,1}... | collective-permute-start | bytes 786440 | tf_op jit(solution)/shard_map/ppermute | solution.py:111
  99.3 15.2 %collective-permute-start.11 = (bf16[256,512]{1,0:T(8,128)(2,1)S(1)}, bf16[256,512]{1,0:T(8,128)(2,1)S(1)}, u32[]{:S(2)}, u32[]{:S(2)}) collective-permute-start(bf16[256,512]{1,0:T(8,128)(2,1)S(1)} %collective-permute-done.10.p2), channel_id=1, source_target_pairs={{0,14},{2,0},{4,2},{6,4},{8,6},{10,8},{12,10},{14,12},{1,3},{3,5},... | collective-permute-start | bytes 786440 | tf_op jit(solution)/shard_map/ppermute | solution.py:111
  106.1 14.0 %collective-permute-start.13 = (bf16[256,512]{1,0:T(8,128)(2,1)S(1)}, bf16[256,512]{1,0:T(8,128)(2,1)S(1)}, u32[]{:S(2)}, u32[]{:S(2)}) collective-permute-start(bf16[256,512]{1,0:T(8,128)(2,1)S(1)} %collective-permute-done.12.p6), channel_id=1, source_target_pairs={{0,4},{2,6},{4,8},{6,10},{8,12},{10,14},{12,0},{14,2},{1,13},{3,15... | collective-permute-start | bytes 786440 | tf_op jit(solution)/shard_map/ppermute | solution.py:111
  110.2 12.2 %collective-permute-start.14 = (bf16[256,512]{1,0:T(8,128)(2,1)S(1)}, bf16[256,512]{1,0:T(8,128)(2,1)S(1)}, u32[]{:S(2)}, u32[]{:S(2)}) collective-permute-start(bf16[256,512]{1,0:T(8,128)(2,1)S(1)} %collective-permute-done.12.p6), channel_id=1, source_target_pairs={{0,2},{2,4},{4,6},{6,8},{8,10},{10,12},{12,14},{14,0},{1,15},{3,1}... | collective-permute-start | bytes 786440 | tf_op jit(solution)/shard_map/ppermute | solution.py:111
  123.3 7.8 %collective-permute-start.17 = (f32[256,512]{1,0:T(8,128)S(1)}, f32[256,512]{1,0:T(8,128)S(1)}, u32[]{:S(2)}, u32[]{:S(2)}) collective-permute-start(f32[256,512]{1,0:T(8,128)S(1)} %shard_map.97), channel_id=1, source_target_pairs={{0,1},{1,0},{2,3},{3,2},{4,5},{5,4},{6,7},{7,6},{8,9},{9,8},{10,11... | collective-permute-start | bytes 1572872 | tf_op jit(solution)/shard_map/ppermute | solution.py:115
  129.5 1.6 %copy-start.1 = (bf16[512,512]{1,0:T(8,128)(2,1)S(1)}, bf16[512,512]{1,0:T(8,128)(2,1)}, u32[]{:S(2)}) copy-start(bf16[512,512]{1,0:T(8,128)(2,1)} %w_message.3) | copy-start | bytes 1572868
